TPU v7x, 32 devices: a whole 2x2x4 slice. The times are simulated.
32 devices in a mesh: dp: 4 (over y, x), fsdp: 8 (over z, core).
Axes of the slice: x: 2, y: 2, z: 4, core: 2. Of those that a mesh axis runs over, the one named last changes fastest.
Arguments:
- tokens: bfloat16 [32768, 1024], P(('dp', 'fsdp')), may hold values from -6 to 6
- cotangent: bfloat16 [32768, 1024], P(('dp', 'fsdp')), may hold values from -15 to 15
- clip_frames: int32 [32, 4], P(('dp', 'fsdp')), may hold values from 0 to 4, as said below
- levels: int32 [128], P(('dp', 'fsdp')), may hold values from 0 to 999
- pad_mask: int32 [32768], P(('dp', 'fsdp')), may hold values from 0 to 1, as said below
- w_mod: bfloat16 [1024, 6144], P(('dp', 'fsdp')), may hold values from -0.1875 to 0.1875
- b_mod: bfloat16 [6144], P(('dp', 'fsdp')), may hold values from -3 to 3
- w_qkv: bfloat16 [1024, 3072], P(('dp', 'fsdp')), may hold values from -0.1875 to 0.1875
- b_qkv: bfloat16 [3072], P(('dp', 'fsdp')), may hold values from -3 to 3
- w_out: bfloat16 [1024, 1024], P(('dp', 'fsdp')), may hold values from -3 to 3
- b_out: bfloat16 [1024], P(('dp', 'fsdp')), may hold values from -3 to 3
- w_up: bfloat16 [1024, 4096], P(('dp', 'fsdp')), may hold values from -0.1875 to 0.1875
- b_up: bfloat16 [4096], P(('dp', 'fsdp')), may hold values from -3 to 3
- w_down: bfloat16 [4096, 1024], P(('dp', 'fsdp')), may hold values from -0.09375 to 0.09375
- b_down: bfloat16 [1024], P(('dp', 'fsdp')), may hold values from -3 to 3
- noise_table: bfloat16 [1024, 1000], P(('dp', 'fsdp')), may hold values from -6 to 6
Outputs:
- block_out: bfloat16 [32768, 1024], P(('dp', 'fsdp'))
- token_grad: bfloat16 [32768, 1024], P(('dp', 'fsdp'))
- wmod_grad: float32 [1024, 6144], P(('dp', 'fsdp'))
- bmod_grad: float32 [6144], P(('dp', 'fsdp'))
- wqkv_grad: float32 [1024, 3072], P(('dp', 'fsdp'))
- bqkv_grad: float32 [3072], P(('dp', 'fsdp'))
- wout_grad: float32 [1024, 1024], P(('dp', 'fsdp'))
- bout_grad: float32 [1024], P(('dp', 'fsdp'))
- wup_grad: float32 [1024, 4096], P(('dp', 'fsdp'))
- bup_grad: float32 [4096], P(('dp', 'fsdp'))
- wdown_grad: float32 [4096, 1024], P(('dp', 'fsdp'))
- bdown_grad: float32 [1024], P(('dp', 'fsdp'))
- table_grad: float32 [1024, 1000], P(('dp', 'fsdp'))
Inputs may be any that keep to these rules, and one draw needn't show every extreme that they name: `clip_frames`: each row sums to 4, its nonzero entries come first; in every draw some device's row is one clip of 4 frames. `pad_mask`: the first of the 256 tokens of every frame is live.
All inputs are finite; a program needn't handle non-finite values.
Results may differ from a plain program's by a relative error of at most 0.013.
The roundings to bfloat16 on the way count: a program that leaves them out, or rounds other values in their place, can miss the bound.
Values may be sent and summed in bfloat16 or wider, within the bound.
A program may use at most 256 MiB of HBM per device.

v0:
```python
import jax
import jax.numpy as jnp
from jax import lax
from jax.experimental import pallas as pl
from jax.experimental.pallas import tpu as pltpu
from jax.sharding import PartitionSpec as P

bf16 = jnp.bfloat16
f32 = jnp.float32
AXES = ("dp", "fsdp")
HD = 64
LANE = 128
EPS = 1e-06
NN = (((1,), (0,)), ((), ()))
NT = (((1,), (1,)), ((), ()))
TN = (((0,), (0,)), ((), ()))


def dot(left, right, dims):
    return lax.dot_general(left, right, dims, preferred_element_type=f32)


def lanes(shape):
    return lax.broadcasted_iota(jnp.int32, shape, 1)


def normalize(values):
    centred = values - jnp.mean(values, axis=1, keepdims=True)
    inverse = lax.rsqrt(jnp.mean(centred * centred, axis=1, keepdims=True) + EPS)
    return centred * inverse, inverse


def normalize_back(grad, normed, inverse):
    return inverse * (
        grad
        - jnp.mean(grad, axis=1, keepdims=True)
        - normed * jnp.mean(grad * normed, axis=1, keepdims=True)
    )


def col_sum(values):
    return jnp.sum(values.astype(f32), axis=0, keepdims=True)


def partner(values):
    return jnp.where(
        lanes(values.shape) % HD < HD // 2,
        pltpu.roll(values, LANE - HD // 2, 1),
        pltpu.roll(values, HD // 2, 1),
    )


def carry_lanes(values):
    sub = lanes(values.shape) % HD
    high = values.astype(bf16).astype(f32)
    rest = values - high
    mid = rest.astype(bf16).astype(f32)
    return jnp.where(
        sub == 8, high, jnp.where(sub == 9, mid, jnp.where(sub == 10, rest - mid, 0.0))
    )


def qkv_kernel(x_ref, mod_ref, w_ref, b_ref, cos_ref, sin_ref, act_ref, q_ref, k_ref, v_ref):
    normed, _ = normalize(x_ref[...].astype(f32))
    act = (normed * (1.0 + mod_ref[0, 1:2, :]) + mod_ref[0, 0:1, :]).astype(bf16)
    act_ref[...] = act
    width = x_ref.shape[1]
    cosine, sine = cos_ref[...], sin_ref[...]
    step = 2 * LANE
    for col in range(0, 3 * width, step):
        raw = dot(act, w_ref[:, col : col + step], NN) + b_ref[:, col : col + step].astype(f32)
        for sub in range(0, step, LANE):
            part = raw[:, sub : sub + LANE]
            at = (col + sub) % width
            if col < width:
                part = (part * cosine + partner(part) * sine).astype(bf16)
                q_ref[:, at : at + LANE] = (part.astype(f32) * 0.125).astype(bf16)
            elif col < 2 * width:
                k_ref[:, at : at + LANE] = (part * cosine + partner(part) * sine).astype(bf16)
            else:
                v_ref[:, at : at + LANE] = part.astype(bf16)


def attention_forward(q_ref, k_ref, v_ref, see_ref, hot_ref, out_ref, aug_ref, *, frames):
    rows_all = q_ref.shape[0]
    size = rows_all // frames
    low = lanes((rows_all, LANE)) < HD
    low_b = lanes((size, LANE)) < HD
    k, v, see = k_ref[...], v_ref[...], see_ref[...]
    one = jnp.ones_like(v)
    keys = (jnp.where(low, k, see), jnp.where(low, see, k))
    vals = (jnp.where(low, v, one), jnp.where(low, one, v))
    for i in range(frames):
        rows = slice(i * size, (i + 1) * size)
        width = (i + 1) * size
        q, hot = q_ref[rows, :], hot_ref[rows, :]
        query = (jnp.where(low_b, q, hot), jnp.where(low_b, hot, q))
        tops, outs = [], []
        for h in range(2):
            scores = dot(query[h], keys[h][:width], NT)
            top = jnp.max(scores, axis=1, keepdims=True)
            expo = jnp.exp(scores - top).astype(bf16)
            outs.append(dot(expo, vals[h][:width], NN))
            tops.append(top)
        num = jnp.where(low_b, outs[0], outs[1])
        den = jnp.where(low_b, outs[1], outs[0])
        out_ref[rows, :] = (num / pltpu.roll(den, HD, 1)).astype(bf16)
        lse = jnp.where(low_b, tops[1], tops[0]) + jnp.log(den)
        aug_ref[rows, :] = (carry_lanes(-lse) + hot.astype(f32)).astype(bf16)


def project_kernel(att_ref, x_ref, mod_ref, w_ref, b_ref, middle_ref, attn_ref, act_ref):
    attn = dot(att_ref[...], w_ref[...].reshape(-1, w_ref.shape[-1]), NN) + b_ref[...].astype(f32)
    attn_ref[...] = attn.astype(bf16)
    middle = x_ref[...].astype(f32) + mod_ref[0, 2:3, :] * attn
    middle_ref[...] = middle
    normed, _ = normalize(middle)
    act_ref[...] = (normed * (1.0 + mod_ref[0, 4:5, :]) + mod_ref[0, 3:4, :]).astype(bf16)


def up_kernel(act_ref, w_ref, b_ref, out_ref, slope_ref):
    hidden = dot(act_ref[...], w_ref[...].reshape(-1, w_ref.shape[-1]), NN) + b_ref[...].astype(f32)
    share = 0.5 * (1.0 + lax.erf(hidden * 0.7071067811865476))
    out_ref[...] = (hidden * share).astype(bf16)
    slope = share + hidden * jnp.exp(-0.5 * hidden * hidden) * 0.3989422804014327
    slope_ref[...] = slope.astype(bf16)


def down_kernel(
    act_ref, w_ref, b_ref, mid_ref, cot_ref, mod_ref, out_ref, dbr_ref, gate_ref, sum_ref, acc_ref
):
    step, last = pl.program_id(0), pl.num_programs(0) - 1
    part = dot(act_ref[...], w_ref[...], NN)

    @pl.when(step == 0)
    def _():
        acc_ref[...] = part

    @pl.when(step > 0)
    def _():
        acc_ref[...] += part

    @pl.when(step == last)
    def _():
        frames = mod_ref.shape[0]
        size = acc_ref.shape[0] // frames
        total = jnp.zeros((1, acc_ref.shape[1]), f32)
        for i in range(frames):
            rows = slice(i * size, (i + 1) * size)
            gate = mod_ref[i, 5:6, :]
            branch = acc_ref[rows, :] + b_ref[...].astype(f32)
            out_ref[rows, :] = (mid_ref[rows, :] + gate * branch).astype(bf16)
            upstream = cot_ref[rows, :].astype(f32)
            d_branch = (upstream * gate).astype(bf16)
            dbr_ref[rows, :] = d_branch
            gate_ref[i : i + 1, :] = col_sum(upstream * branch)
            total += col_sum(d_branch)
        sum_ref[...] = total


def hidden_back_kernel(dbr_ref, w_ref, slope_ref, out_ref, sum_ref):
    d_hidden = (dot(dbr_ref[...], w_ref[...], NT) * slope_ref[...].astype(f32)).astype(bf16)
    out_ref[...] = d_hidden
    sum_ref[...] = col_sum(d_hidden)


def mlp_back_kernel(
    dh_ref, w_ref, mid_ref, cot_ref, attn_ref, mod_ref, dmid_ref, datt_ref, stat_ref, sum_ref, acc_ref, step, last
):
    part = dot(dh_ref[...], w_ref[...], NT)

    @pl.when(step == 0)
    def _():
        acc_ref[...] = part

    @pl.when(step > 0)
    def _():
        acc_ref[...] += part

    @pl.when(step == last)
    def _():
        frames = mod_ref.shape[0]
        size = acc_ref.shape[0] // frames
        total = jnp.zeros((1, acc_ref.shape[1]), f32)
        for i in range(frames):
            rows = slice(i * size, (i + 1) * size)
            d_act = acc_ref[rows, :]
            normed, inverse = normalize(mid_ref[rows, :])
            stat_ref[i, 1:2, :] = col_sum(d_act)
            stat_ref[i, 2:3, :] = col_sum(d_act * normed)
            d_middle = cot_ref[rows, :].astype(f32) + normalize_back(
                d_act * (1.0 + mod_ref[i, 4:5, :]), normed, inverse
            )
            dmid_ref[rows, :] = d_middle
            stat_ref[i, 0:1, :] = col_sum(d_middle * attn_ref[rows, :].astype(f32))
            d_attn = (d_middle * mod_ref[i, 2:3, :]).astype(bf16)
            datt_ref[rows, :] = d_attn
            total += col_sum(d_attn)
        sum_ref[...] = total


def at_columns(ref, index, size):
    return ref.at[:, pl.ds(pl.multiple_of(index * size, size), size)]


def mlp_kernel(
    dbr_ref, wdown_ref, slope_ref, act_ref, wup_ref, mid_ref, cot_ref, attn_ref, mod_ref,
    bup_ref, out_ref, dmid_ref, datt_ref, stat_ref, sum_ref, dh_ref, acc_ref, *, tiles, deep,
):
    step = pl.program_id(0)
    size, wide = dh_ref.shape[1] // tiles, dh_ref.shape[1] // deep

    @pl.when(step < tiles)
    def _():
        hidden_back_kernel(dbr_ref, wdown_ref, slope_ref, at_columns(dh_ref, step, size), bup_ref)

    @pl.when((step >= tiles) & (step < 2 * tiles))
    def _():
        weight_grad_kernel(act_ref, at_columns(dh_ref, step - tiles, size), out_ref)

    @pl.when(step >= 2 * tiles)
    def _():
        mlp_back_kernel(
            at_columns(dh_ref, step - 2 * tiles, wide), wup_ref, mid_ref, cot_ref, attn_ref, mod_ref,
            dmid_ref, datt_ref, stat_ref, sum_ref, acc_ref, step - 2 * tiles, deep - 1,
        )


def attention_back_kernel(
    da_ref, wout_ref, att_ref, q_ref, k_ref, v_ref, o_ref, aug_ref, see_ref, cos_ref, sin_ref, act_ref,
    gout_ref, out_ref, bias_ref, gqkv_ref, do_ref, dp_ref, acc_ref, *, frames, lead, pairs,
):
    step = pl.program_id(0)

    @pl.when(step < lead)
    def _():
        attended_back_kernel(
            da_ref, wout_ref, att_ref, at_columns(do_ref, step, do_ref.shape[1] // lead), gout_ref
        )

    @pl.when((step >= lead) & (step < lead + pairs))
    def _():
        at = step - lead
        attention_backward(
            q_ref, k_ref, v_ref, at_columns(do_ref, at, LANE), o_ref, aug_ref, see_ref, cos_ref, sin_ref,
            out_ref, bias_ref, acc_ref, frames=frames,
        )
        for i in range(3):
            dp_ref[i, :, pl.ds(pl.multiple_of(at * LANE, LANE), LANE)] = out_ref[i]

    @pl.when(step >= lead + pairs)
    def _():
        gqkv_ref[0] = dot(act_ref[...], dp_ref[step - lead - pairs], TN).astype(bf16)


def forward_kernel(
    x_ref, mod_ref, w_ref, b_ref, cos_ref, sin_ref, see_ref, hot_ref, again_ref, mod_again_ref, bout_ref, bup_ref,
    act_ref, q_ref, k_ref, v_ref, att_ref, aug_ref, middle_ref, attn_ref, act_two_ref, up_ref, slope_ref,
    q_all, k_all, v_all, att_all, act_all, *, frames, pairs, tiles, gathers,
):
    step = pl.program_id(0)
    size = x_ref.shape[0]
    marks = (frames, frames + pairs, 2 * frames + pairs)

    @pl.when(step < marks[0])
    def _():
        qkv_kernel(x_ref, mod_ref, w_ref, b_ref, cos_ref, sin_ref, act_ref, q_ref, k_ref, v_ref)
        rows = pl.ds(pl.multiple_of(step * size, size), size)
        for ref, every in ((q_ref, q_all), (k_ref, k_all), (v_ref, v_all)):
            every[rows, :] = ref[...]

    @pl.when((step >= marks[0]) & (step < marks[1]))
    def _():
        at = step - marks[0]
        q, k, v = [at_columns(ref, at, LANE) for ref in (q_all, k_all, v_all)]
        attention_forward(q, k, v, see_ref, hot_ref, att_ref, aug_ref, frames=frames)
        att_all[:, pl.ds(pl.multiple_of(at * LANE, LANE), LANE)] = att_ref[...]

    @pl.when((step >= marks[1]) & (step < marks[2]))
    def _():
        rows = pl.ds(pl.multiple_of((step - marks[1]) * size, size), size)
        weight = gathers[0].refs[3]
        project_kernel(
            att_all.at[rows, :], again_ref, mod_again_ref, weight, bout_ref, middle_ref, attn_ref, act_two_ref
        )
        act_all[rows, :] = act_two_ref[...]

    @pl.when(step >= marks[2])
    def _():
        width = up_ref.shape[1]
        at = pl.multiple_of((step - marks[2]) * width, width)
        up_kernel(act_all, gathers[1].refs[3].at[:, :, :, :, :, pl.ds(at, width)], bup_ref, up_ref, slope_ref)


def attention_backward(
    q_ref, k_ref, v_ref, do_ref, o_ref, aug_ref, see_ref, cos_ref, sin_ref, out_ref, sum_ref, acc_ref, *, frames
):
    rows_all = q_ref.shape[0]
    size = rows_all // frames
    low = lanes((rows_all, LANE)) < HD
    q, aug, grad = q_ref[...], aug_ref[...], do_ref[...]
    prod = grad.astype(f32) * o_ref[...].astype(f32)
    delta_low = jnp.sum(jnp.where(low, prod, 0.0), axis=1, keepdims=True)
    delta_high = jnp.sum(jnp.where(low, 0.0, prod), axis=1, keepdims=True)
    grad_aug = carry_lanes(jnp.where(low, -delta_high, -delta_low)).astype(bf16)
    query = (jnp.where(low, q, aug), jnp.where(low, aug, q))
    upper = (jnp.where(low, grad, grad_aug), jnp.where(low, grad_aug, grad))
    low_b = lanes((size, LANE)) < HD
    sub = lanes((size, LANE)) % HD
    ones = jnp.where((sub >= 8) & (sub <= 10), 1.0, 0.0).astype(bf16)
    sum_k = sum_v = jnp.zeros((1, LANE), f32)
    for j in range(frames):
        rows = slice(j * size, (j + 1) * size)
        start = j * size
        k, v, see = k_ref[rows, :], v_ref[rows, :], see_ref[rows, :] + ones
        keys = (jnp.where(low_b, k, see), jnp.where(low_b, see, k))
        vals = (jnp.where(low_b, v, ones), jnp.where(low_b, ones, v))
        dvs, dks, dqs = [], [], []
        for h in range(2):
            probs = jnp.exp(dot(keys[h], query[h][start:], NT))
            d_scores = (probs * dot(vals[h], upper[h][start:], NT)).astype(bf16)
            dvs.append(dot(probs.astype(bf16), grad[start:], NN))
            dks.append(dot(d_scores, q[start:], NN))
            dqs.append(dot(d_scores, k, TN))
        d_value = jnp.where(low_b, dvs[0], dvs[1]).astype(bf16)
        d_key = jnp.where(low_b, dks[0], dks[1])
        d_key = (d_key * cos_ref[rows, :] - partner(d_key) * sin_ref[rows, :]).astype(bf16)
        out_ref[1, rows, :] = d_key
        out_ref[2, rows, :] = d_value
        sum_k = sum_k + col_sum(d_key)
        sum_v = sum_v + col_sum(d_value)
        d_query = jnp.where(lanes(dqs[0].shape) < HD, dqs[0], dqs[1])
        if j == 0:
            acc_ref[...] = d_query
        else:
            acc_ref[start:, :] += d_query
    d_query = acc_ref[...] * 0.125
    d_query = (d_query * cos_ref[...] - partner(d_query) * sin_ref[...]).astype(bf16)
    out_ref[0] = d_query
    sum_ref[0, 0:1, :] = col_sum(d_query)
    sum_ref[0, 1:2, :] = sum_k
    sum_ref[0, 2:3, :] = sum_v


def input_back_kernel(dp_ref, w_ref, x_ref, dmid_ref, mod_ref, out_ref, stat_ref, acc_ref):
    step, last = pl.program_id(0), pl.num_programs(0) - 1
    part = dot(dp_ref[0], w_ref[...], NT)

    @pl.when(step == 0)
    def _():
        acc_ref[...] = part

    @pl.when(step > 0)
    def _():
        acc_ref[...] += part

    @pl.when(step == last)
    def _():
        frames = mod_ref.shape[0]
        size = acc_ref.shape[0] // frames
        for i in range(frames):
            rows = slice(i * size, (i + 1) * size)
            d_act = acc_ref[rows, :]
            normed, inverse = normalize(x_ref[rows, :].astype(f32))
            stat_ref[i, 0:1, :] = col_sum(d_act)
            stat_ref[i, 1:2, :] = col_sum(d_act * normed)
            back = normalize_back(d_act * (1.0 + mod_ref[i, 1:2, :]), normed, inverse)
            out_ref[rows, :] = (dmid_ref[rows, :] + back).astype(bf16)


def modulation_kernel(small_ref, table_ref, w_ref, part_ref, levels_ref, frames):
    ndev = part_ref.shape[0] * part_ref.shape[1] * part_ref.shape[2] * 2
    rows = levels_ref[...].reshape(ndev, levels_ref.shape[-2], LANE)
    spots = jnp.sum(rows[:, :8], axis=0).astype(jnp.int32)
    count = 2 * frames * ndev
    level = jnp.concatenate([spots[i : i + 1, :] for i in range(count // LANE)], axis=1)
    slot = lax.broadcasted_iota(jnp.int32, (table_ref.shape[1], count), 0)
    hot = jnp.where(slot == level, 1.0, 0.0).astype(bf16)
    embedded = dot(table_ref[...], hot, NN)
    cond = (embedded / (1.0 + jnp.exp(-embedded))).astype(bf16)
    half = part_ref.shape[-1]
    first = lax.broadcasted_iota(jnp.int32, (count, 1), 0) % (2 * frames) < frames
    step = 512
    for col in range(0, half, step):
        low = dot(cond, w_ref[:, col : col + step], TN)
        high = dot(cond, w_ref[:, half + col : half + col + step], TN)
        value = jnp.where(first, low, high)
        part_ref[..., col : col + step] = value.reshape(part_ref.shape[:-1] + (step,)).astype(part_ref.dtype)


def weight_grad_kernel(left_ref, right_ref, out_ref):
    out_ref[...] = dot(left_ref[...], right_ref[...], TN).astype(bf16)


def attended_back_kernel(da_ref, w_ref, att_ref, datt_ref, out_ref):
    datt_ref[...] = dot(da_ref[...], w_ref[...], NT).astype(bf16)
    out_ref[...] = dot(att_ref[...], da_ref[...], TN).astype(bf16)


def qkv_grad_kernel(left_ref, right_ref, out_ref):
    out_ref[0] = dot(left_ref[...], right_ref[0], TN).astype(bf16)


def like(shape, kind):
    return jax.ShapeDtypeStruct(shape, kind)


def whole(shape):
    return pl.BlockSpec(shape, lambda i: (0,) * len(shape))


def by_rows(size, width):
    return pl.BlockSpec((size, width), lambda i: (i, 0))


def by_cols(height, size):
    return pl.BlockSpec((height, size), lambda i: (0, i))


MESH = pl.DeviceIdType.MESH
ANY = pl.BlockSpec(memory_space=pl.ANY)
VMEM = pl.BlockSpec(memory_space=pltpu.VMEM)
DMA = pltpu.SemaphoreType.DMA


class Place:
    def __init__(self, sizes):
        self.ny, self.nx, self.nz = sizes
        self.half = self.nz // 2
        self.rest = self.nz - self.half
        self.low, self.high = pl.ds(0, self.half), pl.ds(self.half, self.rest)
        self.dp, self.fsdp = lax.axis_index("dp"), lax.axis_index("fsdp")
        self.y, self.x = lax.div(self.dp, self.nx), lax.rem(self.dp, self.nx)
        self.z, self.c = lax.div(self.fsdp, 2), lax.rem(self.fsdp, 2)

        self.shifts, self.devices = {}, {}
        for axis, size in dict(y=self.ny, x=self.nx, z=self.nz, c=2).items():
            for k in range(1, size):
                at = lax.rem(getattr(self, axis) + k, size)
                self.shifts[axis, k] = self.shifts[axis, k - size] = at
                self.devices[axis, k] = dict(
                    y=(at * self.nx + self.x, self.fsdp), x=(self.y * self.nx + at, self.fsdp),
                    z=(self.dp, at * 2 + self.c), c=(self.dp, self.z * 2 + at),
                )[axis]
        self.other = self.shifts["c", 1]
        self.nd, self.nf = self.ny * self.nx, self.nz * 2
        for k in range(1, self.nd):
            at = lax.rem(self.dp + k, self.nd)
            self.shifts["d", k] = self.shifts["d", k - self.nd] = at
            self.devices["d", k] = (at, self.fsdp)
        for k in range(1, self.nf):
            at = lax.rem(self.fsdp + k, self.nf)
            self.shifts["f", k] = self.shifts["f", k - self.nf] = at
            self.devices["f", k] = (self.dp, at)

    def shift(self, axis, k):
        return self.shifts[axis, k]

    def device(self, axis, k):
        return self.devices[axis, k]

    def enter(self, axes):
        barrier = pltpu.get_barrier_semaphore()
        sizes = dict(y=self.ny, x=self.nx, z=self.nz, c=2, d=self.nd, f=self.nf)
        count = 0
        for axis in axes:
            for k in range(1, sizes[axis]):
                count += 1
                pl.semaphore_signal(barrier, inc=1, device_id=self.device(axis, k), device_id_type=MESH)
        pl.semaphore_wait(barrier, count)


class Move:
    ins, in_specs, outs, out_specs, scratch, aliases = (), (), (), (), (), ()

    def bind(self, place, ins, outs, scratch):
        self.place, self.in_refs, self.out_refs, self.refs = place, ins, outs, scratch
        self.slots, self.local_slots, self.legs = {}, {}, []

    def copy(self, key, src, dst, axis, k):
        slot = self.slots.setdefault(key, len(self.slots))
        return pltpu.make_async_remote_copy(
            src_ref=src, dst_ref=dst, send_sem=self.refs[0].at[slot], recv_sem=self.refs[1].at[slot],
            device_id=self.place.device(axis, k), device_id_type=MESH,
        )

    def start(self, items):
        for item in items:
            self.copy(*item).start()

    def arrived(self, key, dst, axis, k):
        self.copy(key, dst, dst, axis, k).wait_recv()

    def drain(self, items):
        for item in items:
            self.copy(*item).wait_send()

    def local(self, key, src, dst):
        slot = self.local_slots.setdefault(key, len(self.local_slots))
        return pltpu.make_async_copy(src, dst, self.refs[2].at[slot])


class Held:
    def __init__(self, shape, kind):
        self.shape, self.dtype, self.ref = shape, kind, None


def part_of(ref, part, core):
    if part is None:
        return ref.at[:, :, :, core]
    if isinstance(part, int):
        return ref.at[part, :, :, :, core]
    return ref.at[:, :, :, core, :, part[0] : part[1]]


def block_of(array, part):
    rows, columns = array.shape[-2:]
    return (rows, part[1] - part[0]) if isinstance(part, tuple) else (rows, columns)


def legs_copies(sizes):
    ny, nx, nz = sizes
    return (nz - 1) + 4 * (nx - 1) + 4 * (ny - 1) + 1


class Gather(Move):
    def __init__(self, sizes, array, actions, begun=False, shard=None, load=False):
        ny, nx, nz = sizes
        self.begun, self.actions = begun, actions
        self.held = array if isinstance(array, Held) else None
        self.ins, self.in_specs = ([], []) if self.held else ([array], [ANY if begun else VMEM])
        if shard is not None:
            self.ins, self.in_specs = [array, shard], [ANY, VMEM]
        shape = array.shape if begun else (ny, nx, nz, 2) + array.shape
        self.outs, self.out_specs = [like(shape, array.dtype)], [ANY]
        parts = len({what[2:] for _, what in actions}) if actions else 3
        self.scratch = [DMA((legs_copies(sizes) * parts,)), DMA((legs_copies(sizes) * parts,)), DMA((parts + 3,))]
        if load:
            self.scratch.append(pltpu.VMEM(shape, array.dtype))
        self.aliases = [(0, 0)] if begun else []

    def act(self, what):
        if what[0] in "ld":
            part = what[1:]
            copy = self.local(("load", part), self.spot((slice(None),) * 4, part), self.held_part(part))
            return copy.start() if what[0] == "l" else copy.wait()
        op, leg, part = what[0], int(what[1]), what[2:]
        if op != "s":
            self.wait_leg(leg, part)
        if op != "w":
            self.start_leg(leg + (op == "n"), part)
        else:
            for each in self.legs:
                if each[1] == part:
                    self.drain(self.leaving(*each))

    def columns(self, part):
        width = self.out_refs[0].shape[-1]
        half = width // 2
        return {"": slice(None), "a": slice(0, half), "b": slice(half, width)}[part]

    def held_part(self, part):
        return self.refs[3].at[:, :, :, :, :, self.columns(part)]

    def spot(self, index, part):
        return self.out_refs[0].at[index + (slice(None), self.columns(part))]

    def items(self, leg):
        p, full = self.place, self.out_refs[0]
        y, x, z, c = p.y, p.x, p.z, p.c
        d = p.other
        xs, ys, zs = range(1, p.nx), range(1, p.ny), range(1, p.nz)
        back = p.shift
        if leg == 0:
            return [(("z", k), (y, x, z, c), (y, x, back("z", -k), c), "z", k) for k in zs]
        if leg == 1:
            return (
                [(("x", k), (y, x, p.low, c), (y, back("x", -k), p.low, c), "x", k) for k in xs]
                + [(("y", k), (y, x, p.high, c), (back("y", -k), x, p.high, c), "y", k) for k in ys]
                + [("c", (y, x, slice(None), c), (y, x, slice(None), d), "c", 1)]
            )
        every = slice(None)
        if leg == 2:
            return (
                [(("xy", k), (y, every, p.low, c), (back("y", -k), every, p.low, c), "y", k) for k in ys]
                + [(("yx", k), (every, x, p.high, c), (every, back("x", -k), p.high, c), "x", k) for k in xs]
                + [(("cx", k), (y, back("x", -k), p.low, c), (y, back("x", -k), p.low, d), "c", 1) for k in xs]
                + [(("cy", k), (back("y", -k), x, p.high, c), (back("y", -k), x, p.high, d), "c", 1) for k in ys]
            )
        return [
            (("cxy", k), (back("y", -k), every, p.low, c), (back("y", -k), every, p.low, d), "c", 1) for k in ys
        ] + [(("cyx", k), (every, back("x", -k), p.high, c), (every, back("x", -k), p.high, d), "c", 1) for k in xs]

    def source(self):
        return self.held.ref if self.held else self.in_refs[-1]

    def own(self, part):
        p = self.place
        mine = self.source().at[:, self.columns(part)]
        return self.local(part, mine, self.spot((p.y, p.x, p.z, p.c), part))

    def leaving(self, leg, part):
        for key, leaves, _, axis, k in self.items(leg):
            to = self.spot(leaves, part)
            yield (key, part), self.source().at[:, self.columns(part)] if leg == 0 else to, to, axis, k

    def start_leg(self, leg, part):
        self.legs.append((leg, part))
        if leg == 0:
            self.own(part).start()
        self.start(self.leaving(leg, part))

    def wait_leg(self, leg, part):
        if leg == 0:
            self.own(part).wait()
        for key, _, arrives, axis, k in self.items(leg):
            self.arrived((key, part), self.spot(arrives, part), axis, k)


class Spread(Move):
    def __init__(self, sizes, array):
        ny, nx, nz = sizes
        self.ins, self.in_specs = [array], [VMEM]
        self.outs, self.out_specs = [like((ny * nx, 2 * nz) + array.shape, array.dtype)], [ANY]
        count = DMA((ny * nx + 2 * nz - 2,))
        self.scratch, self.actions = [count, count, DMA((1,))], ()

    def act(self, what):
        p, full = self.place, self.out_refs[0]
        own = ("own", self.in_refs[0], full.at[p.dp, p.fsdp])
        along = [(("f", k), self.in_refs[0], full.at[p.dp, p.fsdp], "f", k) for k in range(1, p.nf)]
        across = [(("d", k), full.at[p.dp], full.at[p.dp], "d", k) for k in range(1, p.nd)]
        if what == "0":
            self.local(*own).start()
            self.start(along)
        elif what == "1":
            self.local(*own).wait()
            for k in range(1, p.nf):
                self.arrived(("f", k), full.at[p.dp, p.shift("f", -k)], "f", k)
            self.start(across)
        else:
            for k in range(1, p.nd):
                self.arrived(("d", k), full.at[p.shift("d", -k)], "d", k)
            self.drain(along + across)


def add_blocks(into, where, counts, terms):
    total = 1
    for n in counts:
        total *= n

    def body(flat, carry):
        at = []
        for n in reversed(counts):
            at.append(lax.rem(flat, n))
            flat = lax.div(flat, n)
        at = tuple(at[::-1])
        spot = where(*at)
        value = into[spot].astype(f32)
        for ref, index in terms(*at):
            value = value + ref[index].astype(f32)
        into[spot] = value.astype(into.dtype)
        return carry

    lax.fori_loop(0, total, body, 0)


class Reduce(Move):
    def __init__(self, sizes, array, actions, part=None):
        self.actions, self.part = actions, part
        ny, nx, nz = sizes
        half, rest = nz // 2, nz - nz // 2
        block, kind = block_of(array, part), array.dtype
        self.held = array if isinstance(array, Held) else None
        self.ins, self.in_specs = ([], []) if self.held else ([array], [ANY])
        self.outs, self.out_specs = [like(block, f32)], [VMEM]
        shapes = [
            (ny, nx, nz), (ny, nx, nz), (ny - 1, nx, half), (nx - 1, ny, rest), (nx - 1, half), (ny - 1, rest), (nz - 1,)
        ]
        count = DMA((1 + 2 * (nx - 1) + 2 * (ny - 1) + nz - 1,))
        self.scratch = [count, count, DMA((1,))] + [pltpu.VMEM(a + block, kind) for a in shapes]

    def act(self, what):
        p, stage = self.place, int(what)
        y, x, z = p.y, p.x, p.z
        source = self.held.ref if self.held else self.in_refs[0]
        acc, core, la, lb, ma, mb, last = self.refs[3:]
        own = ("own", part_of(source, self.part, p.c), acc)
        xs, ys, zs = range(1, p.nx), range(1, p.ny), range(1, p.nz)

        def leaving(at):
            if at == 0:
                return [("c", part_of(source, self.part, p.other), core, "c", 1)]
            if at == 1:
                return [(("y", k), acc.at[p.shift("y", k), :, p.low], la.at[k - 1], "y", k) for k in ys] + [
                    (("x", k), acc.at[:, p.shift("x", k), p.high], lb.at[k - 1], "x", k) for k in xs
                ]
            if at == 2:
                return [(("yx", k), acc.at[y, p.shift("x", k), p.low], ma.at[k - 1], "x", k) for k in xs] + [
                    (("xy", k), acc.at[p.shift("y", k), x, p.high], mb.at[k - 1], "y", k) for k in ys
                ]
            return [(("z", k), acc.at[y, x, p.shift("z", k)], last.at[k - 1], "z", k) for k in zs]

        if stage > 0:
            for key, _, to, axis, k in leaving(stage - 1):
                self.arrived(key, to, axis, k)
        if stage == 0:
            self.local(*own).start()
        elif stage == 1:
            self.local(*own).wait()
            add_blocks(acc, lambda *at: at, (p.ny, p.nx, p.nz), lambda *at: [(core, at)])
        elif stage == 2:
            add_blocks(
                acc, lambda i, j: (y, i, j), (p.nx, p.half), lambda i, j: [(la, (k, i, j)) for k in range(p.ny - 1)]
            )
            add_blocks(
                acc, lambda i, j: (i, x, p.half + j), (p.ny, p.rest),
                lambda i, j: [(lb, (k, i, j)) for k in range(p.nx - 1)],
            )
        elif stage == 3:
            add_blocks(acc, lambda j: (y, x, j), (p.half,), lambda j: [(ma, (k, j)) for k in range(p.nx - 1)])
            add_blocks(
                acc, lambda j: (y, x, p.half + j), (p.rest,), lambda j: [(mb, (k, j)) for k in range(p.ny - 1)]
            )
        if stage < 4:
            self.start(leaving(stage))
        else:
            value = acc[y, x, z].astype(f32)
            for k in range(p.nz - 1):
                value = value + last[k].astype(f32)
            self.out_refs[0][...] = value
            for at in range(4):
                self.drain(leaving(at))


class ReduceCore(Move):
    def __init__(self, sizes, array, actions, part=None):
        self.actions, self.part = actions, part
        ny, nx, nz = sizes
        self.held = array if isinstance(array, Held) else None
        self.ins, self.in_specs = ([], []) if self.held else ([array], [ANY])
        self.outs, self.out_specs = [like((ny, nx, nz) + block_of(array, part), array.dtype)], [ANY]
        self.scratch = [DMA((1,)), DMA((1,))]

    def act(self, what):
        p = self.place
        source = self.held.ref if self.held else self.in_refs[0]
        leaving = [("c", part_of(source, self.part, p.other), self.out_refs[0], "c", 1)]
        if what == "s":
            self.start(leaving)
        else:
            self.arrived("c", self.out_refs[0], "c", 1)
            self.drain(leaving)


class ReduceFirst(Move):
    def __init__(self, sizes, array, core, actions, part=None):
        self.actions, self.part, self.core = actions, part, core
        ny, nx, nz = sizes
        half, rest = nz // 2, nz - nz // 2
        block, kind = block_of(array, part), array.dtype
        self.held = array if isinstance(array, Held) else None
        self.ins = ([] if self.held else [array]) + ([] if isinstance(core, Move) else [core])
        self.in_specs = [ANY] * len(self.ins)
        self.outs = [
            like((ny - 1, nx, half) + block, kind), like((nx - 1, ny, rest) + block, kind),
            like((nx, half) + block, kind), like((ny, rest) + block, kind),
        ]
        self.out_specs = [ANY] * 4
        remote = DMA((nx + ny - 2,))
        self.scratch = [remote, remote, DMA((4,))] + [pltpu.VMEM((ny, nx, nz) + block, kind)] * 2

    def act(self, what):
        p = self.place
        source = self.held.ref if self.held else self.in_refs[0]
        core = self.core.out_refs[0] if isinstance(self.core, Move) else self.in_refs[-1]
        acc, buf = self.refs[3:]
        la, lb, ka, kb = self.out_refs
        loads = [("acc", part_of(source, self.part, p.c), acc), ("buf", core, buf)]
        leaving = [
            (("y", k), acc.at[p.shift("y", k), :, p.low], la.at[k - 1], "y", k) for k in range(1, p.ny)
        ] + [(("x", k), acc.at[:, p.shift("x", k), p.high], lb.at[k - 1], "x", k) for k in range(1, p.nx)]
        keeps = [("ka", acc.at[p.y, :, p.low], ka), ("kb", acc.at[:, p.x, p.high], kb)]
        if what == "l":
            for item in loads:
                self.local(*item).start()
        elif what == "a":
            for item in loads:
                self.local(*item).wait()
            add_blocks(acc, lambda *at: at, (p.ny, p.nx, p.nz), lambda *at: [(buf, at)])
            self.start(leaving)
            for item in keeps:
                self.local(*item).start()
        else:
            for k in range(1, p.ny):
                self.arrived(("y", k), la.at[k - 1], "y", k)
            for k in range(1, p.nx):
                self.arrived(("x", k), lb.at[k - 1], "x", k)
            for item in keeps:
                self.local(*item).wait()
            self.drain(leaving)


class ReduceSecond(Move):
    def __init__(self, sizes, first, actions):
        self.actions, self.first = actions, first
        ny, nx, nz = sizes
        half, rest = nz // 2, nz - nz // 2
        self.inside = isinstance(first, Move)
        arrays = first.outs if self.inside else first
        block, kind = arrays[0].shape[-2:], arrays[0].dtype
        self.ins, self.in_specs = ([], []) if self.inside else (list(arrays), [ANY] * 4)
        self.outs = [
            like((nx - 1, half) + block, kind), like((ny - 1, rest) + block, kind), like((nz,) + block, kind)
        ]
        self.out_specs = [ANY] * 3
        remote = DMA((nx + ny - 2,))
        self.scratch = [remote, remote, DMA((6,))] + [pltpu.VMEM(a.shape, kind) for a in arrays]

    def act(self, what):
        p = self.place
        arrays = self.first.out_refs if self.inside else self.in_refs
        bufs = self.refs[3:]
        la, lb, ka, kb = bufs
        ma, mb, kept = self.out_refs
        loads = [(i, a, b) for i, (a, b) in enumerate(zip(arrays, bufs))]
        leaving = [(("x", k), ka.at[p.shift("x", k)], ma.at[k - 1], "x", k) for k in range(1, p.nx)]
        leaving += [(("y", k), kb.at[p.shift("y", k)], mb.at[k - 1], "y", k) for k in range(1, p.ny)]
        keeps = [("ka", ka.at[p.x], kept.at[p.low]), ("kb", kb.at[p.y], kept.at[p.high])]
        if what == "l":
            for item in loads:
                self.local(*item).start()
        elif what == "a":
            for item in loads:
                self.local(*item).wait()
            add_blocks(ka, lambda *at: at, (p.nx, p.half), lambda i, j: [(la, (k, i, j)) for k in range(p.ny - 1)])
            add_blocks(kb, lambda *at: at, (p.ny, p.rest), lambda i, j: [(lb, (k, i, j)) for k in range(p.nx - 1)])
            self.start(leaving)
            for item in keeps:
                self.local(*item).start()
        else:
            for k in range(1, p.nx):
                self.arrived(("x", k), ma.at[k - 1], "x", k)
            for k in range(1, p.ny):
                self.arrived(("y", k), mb.at[k - 1], "y", k)
            for item in keeps:
                self.local(*item).wait()
            self.drain(leaving)


class ReduceLast(Move):
    def __init__(self, sizes, second, actions):
        self.actions, self.second = actions, second
        ny, nx, nz = sizes
        self.inside = isinstance(second, Move)
        arrays = second.outs if self.inside else second
        block, kind = arrays[0].shape[-2:], arrays[0].dtype
        self.ins, self.in_specs = ([], []) if self.inside else (list(arrays), [ANY] * 3)
        self.outs, self.out_specs = [like(block, f32)], [VMEM]
        self.scratch = [DMA((nz - 1,)), DMA((nz - 1,)), DMA((3,))] + [pltpu.VMEM(a.shape, kind) for a in arrays]
        self.scratch += [pltpu.VMEM((nz - 1,) + block, kind)]

    def act(self, what):
        p = self.place
        arrays = self.second.out_refs if self.inside else self.in_refs
        ma, mb, kept, last = self.refs[3:]
        loads = [(i, a, b) for i, (a, b) in enumerate(zip(arrays, (ma, mb, kept)))]
        leaving = [(("z", k), kept.at[p.shift("z", k)], last.at[k - 1], "z", k) for k in range(1, p.nz)]
        if what == "l":
            for item in loads:
                self.local(*item).start()
        elif what == "a":
            for item in loads:
                self.local(*item).wait()
            add_blocks(kept, lambda j: (j,), (p.half,), lambda j: [(ma, (k, j)) for k in range(p.nx - 1)])
            add_blocks(
                kept, lambda j: (p.half + j,), (p.rest,), lambda j: [(mb, (k, j)) for k in range(p.ny - 1)]
            )
            self.start(leaving)
        else:
            for k in range(1, p.nz):
                self.arrived(("z", k), last.at[k - 1], "z", k)
            value = kept[p.z].astype(f32)
            for k in range(p.nz - 1):
                value = value + last[k].astype(f32)
            self.out_refs[0][...] = value
            self.drain(leaving)


def run(
    kernel, grid, ins, outs, shapes, args, scratch=(), name=None, moves=(), sizes=None, group=None, axes="yxzc", script=None
):
    single = not isinstance(shapes, (list, tuple))
    outs, shapes = ([outs], [shapes]) if single else (list(outs), list(shapes))
    counts = len(ins), len(outs), len(scratch)
    all_ins, all_specs, all_outs = list(args), list(ins), list(shapes)
    all_out_specs, all_scratch, aliases = list(outs), list(scratch), {}
    for move in moves:
        for i, o in move.aliases:
            aliases[len(all_ins) + i] = len(all_outs) + o
        all_ins += list(move.ins)
        all_specs += list(move.in_specs)
        all_outs += list(move.outs)
        all_out_specs += list(move.out_specs)
        all_scratch += list(move.scratch)

    def body(*refs):
        refs = list(refs)

        def take(n):
            part = refs[:n]
            del refs[:n]
            return part

        mine_in = take(counts[0])
        moved_in = [take(len(m.ins)) for m in moves]
        mine_out = take(counts[1])
        moved_out = [take(len(m.outs)) for m in moves]
        mine_scratch = take(counts[2])
        place = Place(sizes) if moves else None
        for move, i, o in zip(moves, moved_in, moved_out):
            move.bind(place, i, o, take(len(move.scratch)))
        step = pl.program_id(0)

        def turn(at):
            for move in moves:
                for when, what in move.actions:
                    if when == at:
                        move.act(what)

        def play():
            for item in script:
                if isinstance(item, tuple):
                    item[0].act(item[1])
                else:
                    item(mine_in, mine_out, mine_scratch)

        if kernel is None:
            place.enter(axes)
            play()
            return

        for at in range(grid):
            if any(when == at for m in moves for when, _ in m.actions):

                @pl.when(step == at)
                def _(at=at):
                    if at == 0:
                        place.enter(axes)
                    turn(at)

        kernel(*mine_in, *mine_out, *mine_scratch)
        if moves:

            @pl.when(step == grid - 1)
            def _():
                turn(grid)
                if script is not None:
                    play()

    params = dict(vmem_limit_bytes=(63 if moves else 60) * 1024 * 1024)
    if moves:
        params.update(collective_id=group, has_side_effects=True)
    moved = sum(a.size * a.dtype.itemsize for a in args)
    results = pl.pallas_call(
        body,
        grid=(grid,),
        in_specs=all_specs,
        out_specs=all_out_specs,
        out_shape=all_outs,
        scratch_shapes=all_scratch,
        input_output_aliases=aliases,
        name=name,
        cost_estimate=pl.CostEstimate(flops=0, bytes_accessed=2 * moved, transcendentals=0),
        compiler_params=pltpu.CompilerParams(**params),
    )(*all_ins)
    return results[0] if single and not moves else results


def tables(clip_row, pad, count):
    frames = clip_row.shape[0]
    size = count // frames
    slots = jnp.arange(frames, dtype=jnp.int32)
    ends = jnp.sum(jnp.where(slots[None, :] <= slots[:, None], clip_row[None, :], 0), axis=1)
    clip_of = jnp.sum((slots[:, None] >= ends[None, :]).astype(jnp.int32), axis=1)
    starts = ends - clip_row
    start_of = jnp.sum(jnp.where(clip_of[:, None] == slots[None, :], starts[None, :], 0), axis=1)
    frame_pos = slots - start_of
    frame = jnp.arange(count, dtype=jnp.int32) // size
    lane = jnp.arange(LANE, dtype=jnp.int32) % HD
    frame_hot = frame[:, None] == lane[None, :]
    own = frame[:, None] == slots[None, :]
    clip_tok = jnp.sum(jnp.where(own, clip_of[None, :], 0), axis=1)
    pos_tok = jnp.sum(jnp.where(own, frame_pos[None, :], 0), axis=1)
    lane_own = lane[:, None] == slots[None, :]
    lane_clip = jnp.sum(jnp.where(lane_own, clip_of[None, :], 0), axis=1)
    lane_pos = jnp.sum(jnp.where(lane_own, frame_pos[None, :], 0), axis=1)
    seen = (
        (clip_tok[:, None] == lane_clip[None, :])
        & (pos_tok[:, None] <= lane_pos[None, :])
        & (pad[:, None] == 1)
    )
    see = jnp.where((lane[None, :] < frames) & ~seen, -1e30, 0.0).astype(bf16)
    quarter = HD // 4
    freq = 10000.0 ** (-jnp.arange(quarter, dtype=f32) / quarter)
    patch = jnp.arange(count, dtype=jnp.int32) % size
    angle = jnp.concatenate(
        [pos_tok.astype(f32)[:, None] * freq[None, :], patch.astype(f32)[:, None] * freq[None, :]],
        axis=1,
    )
    cosine, sine = jnp.cos(angle), jnp.sin(angle)
    cosine = jnp.concatenate([cosine] * 4, axis=1)
    sine = jnp.concatenate([-sine, sine, -sine, sine], axis=1)
    return see, frame_hot.astype(bf16), cosine, sine


def per_device(
    tokens, cotangent, clip_frames, levels, pad_mask, w_mod, b_mod, w_qkv, b_qkv, w_out, b_out,
    w_up, b_up, w_down, b_down, noise_table,
):
    count, width = tokens.shape
    frames = levels.shape[0]
    size = count // frames
    hidden = w_up.shape[1]
    ndev = width // w_up.shape[0]
    me = lax.axis_index("dp") * lax.axis_size("fsdp") + lax.axis_index("fsdp")

    dp, fsdp = lax.axis_size("dp"), lax.axis_size("fsdp")
    sizes = (dp // 2, 2, fsdp // 2)
    lead = sizes + (2,)

    def flat(array):
        return array.reshape(-1, array.shape[-1])

    def blocks(array, front=0):
        rows = array.shape[front] // ndev
        return array.reshape(array.shape[:front] + lead + (rows, array.shape[-1]))

    biases = [b_mod, b_qkv, b_out, b_up, b_down]
    lengths = [b.shape[0] for b in biases]
    spots = jnp.arange(8 * LANE, dtype=jnp.int32)
    mine_at = jnp.where(spots // (2 * frames) == me, jnp.tile(levels, spots.shape[0] // frames), 0)
    packed = jnp.concatenate([mine_at.astype(f32)] + [b.astype(f32) for b in biases])
    packed = jnp.pad(packed, (0, 16 * LANE - packed.shape[0])).reshape(16, LANE)
    table_pad = jnp.pad(noise_table, ((0, 0), (0, -noise_table.shape[1] % LANE)))
    part = Held(lead + (2 * frames, w_mod.shape[1] // 2), bf16)
    small = Spread(sizes, packed)
    qkv_w = Gather(sizes, w_qkv, ())
    out_w, up_w = Gather(sizes, w_out, ()), Gather(sizes, w_up, ())
    mod_sum = Reduce(sizes, part, ())

    def add_modulation(ins, _, scratch):
        part.ref = scratch[0]
        load = pltpu.make_async_copy(small.out_refs[0], scratch[1], scratch[2].at[0])
        load.start()
        load.wait()
        modulation_kernel(None, ins[0], ins[1], scratch[0], scratch[1], frames)

    head = run(
        None, 1, [VMEM] * 2, [], [], [table_pad, w_mod],
        [pltpu.VMEM(part.shape, bf16), pltpu.VMEM(small.outs[0].shape, f32), DMA((1,))], name="head",
        moves=[small, qkv_w, out_w, up_w, mod_sum], sizes=sizes, group=1, axes="df",
        script=[
            (small, "0"), (qkv_w, "s0a"), (qkv_w, "s0b"), (out_w, "s0"), (small, "1"), (small, "2"), add_modulation,
            (mod_sum, "0"), (qkv_w, "n0a"), (mod_sum, "1"), (qkv_w, "n0b"), (mod_sum, "2"), (qkv_w, "n1a"), (mod_sum, "3"),
            (up_w, "s0a"), (qkv_w, "n1b"), (mod_sum, "4"), (qkv_w, "n2a"), (qkv_w, "n2b"), (qkv_w, "w3a"), (qkv_w, "w3b"),
            (out_w, "w0"), (up_w, "w0a"),
        ],
    )
    small, qkv_w, out_w, up_w = head[:4]
    small = small.reshape(ndev, -1)
    all_levels = jnp.sum(small[:, : 8 * LANE], axis=0).reshape(-1, 2 * frames)[:ndev, :frames]
    all_levels = all_levels.reshape(-1).astype(jnp.int32)
    full_bias, at = [], 8 * LANE
    for length in lengths:
        full_bias.append(small[:, at : at + length].reshape(1, -1))
        at += length
    bias_mod, bias_qkv, bias_out, bias_up, bias_down = full_bias
    modulation = jnp.transpose(head[-1].reshape(2, frames, -1), (1, 0, 2)).reshape(frames, -1)
    modulation = (modulation + bias_mod).reshape(frames, 6, width)
    full_qkv = flat(qkv_w)
    see, frame_hot, cosine, sine = tables(clip_frames[0], pad_mask, count)

    acts = like((count, width), bf16)
    wide = like((count, width), f32)
    tall = like((count, hidden), bf16)
    row = whole((1, width))
    mod_row = pl.BlockSpec((1, 6, width), lambda i: (i, 0, 0))
    mod_all = whole((frames, 6, width))
    rows_bf = by_rows(size, width)
    def turn(start, count, index):
        return lambda i: index(jnp.clip(i - start, 0, count - 1))

    def held(shape):
        return pl.BlockSpec(shape, lambda i: (0,) * len(shape), pipeline_mode=pl.Buffered(1))

    pairs = width // LANE
    step = 512
    tiles = hidden // step
    m1, m2 = frames + pairs, 2 * frames + pairs
    steps = m2 + tiles
    rows_one = pl.BlockSpec((size, width), turn(0, frames, lambda i: (i, 0)))
    rows_two = pl.BlockSpec((size, width), turn(m1, frames, lambda i: (i, 0)))
    lanes_one = pl.BlockSpec((size, LANE), turn(0, frames, lambda i: (i, 0)))
    pair_one = pl.BlockSpec((count, LANE), turn(frames, pairs, lambda i: (0, i)))
    cols_one = pl.BlockSpec((count, step), turn(m2, tiles, lambda i: (0, i)))
    move_out = Gather(
        sizes, out_w, [(0, "s1"), (4, "n1"), (8, "n2"), (9, "w3"), (9, "l"), (m1, "d")], True, load=True
    )
    move_up = Gather(
        sizes, up_w,
        [
            (0, "s1a"), (0, "s0b"), (2, "n1a"), (5, "n0b"), (6, "n2a"), (7, "w3a"), (7, "la"), (9, "n1b"), (m2, "da"),
            (m2 + 1, "n2b"), (m2 + 2, "w3b"), (m2 + 2, "lb"), (m2 + tiles // 2, "db"),
        ], True, w_up, True,
    )
    move_down = Gather(
        sizes, w_down,
        [
            (1, "s0a"), (1, "s0b"), (8, "n0a"), (11, "n0b"), (11, "n1a"), (m2 + 3, "n1b"), (steps, "n2a"), (steps, "n2b"),
            (steps, "w3a"), (steps, "w3b"),
        ],
    )
    act_one, query, key, value, attended, aug, middle, attn, act_two, activated, slope, *moved = run(
        lambda *refs: forward_kernel(*refs, frames=frames, pairs=pairs, tiles=tiles, gathers=(move_out, move_up)), steps,
        [
            rows_one, pl.BlockSpec((1, 6, width), turn(0, frames, lambda i: (i, 0, 0))), held((width, 3 * width)),
            held((1, 3 * width)), lanes_one, lanes_one, held((count, LANE)), held((count, LANE)), rows_two,
            pl.BlockSpec((1, 6, width), turn(m1, frames, lambda i: (i, 0, 0))), held((1, width)),
            pl.BlockSpec((1, step), turn(m2, tiles, lambda i: (0, i))),
        ],
        [rows_one] * 4 + [pair_one] * 2 + [rows_two] * 3 + [cols_one] * 2,
        [acts] * 6 + [wide, acts, acts] + [tall] * 2,
        (
            tokens, modulation, full_qkv, bias_qkv, cosine, sine, see, frame_hot, tokens, modulation, bias_out, bias_up,
        ),
        [pltpu.VMEM((count, width), bf16)] * 5, name="fwd",
        moves=[move_out, move_up, move_down], sizes=sizes, group=2,
    )
    full_out, full_up, full_down = [flat(w) for w in moved]
    full = whole((count, width))
    cols_h = by_cols(count, step)
    acc = pltpu.VMEM((count, width), f32)
    deep = hidden // width
    block_out, d_branch, d_gate_two, bdown = run(
        down_kernel, deep, [by_cols(count, width), by_rows(width, width), row, full, full, mod_all],
        [full, full, whole((frames, width)), row],
        [acts, acts, like((frames, width), f32), like((1, width), f32)],
        (activated, full_down, bias_down, middle, cotangent, modulation), [acc], name="down",
    )
    wdown = run(
        weight_grad_kernel, tiles, [cols_h, full], by_rows(step, width), like((hidden, width), bf16),
        (activated, d_branch), name="wdown",
    )
    wdown = blocks(wdown)
    stacked = pl.BlockSpec((1, count, width), lambda i: (i, 0, 0))
    once = held((count, width))
    mod_once = held((frames, 6, width))
    halves = ((0, width // 2), (width // 2, width))
    steps = 2 * tiles + deep
    cores = [ReduceCore(sizes, wdown, [(0, "s"), (2 + 2 * i, "w")], h) for i, h in enumerate(halves)]
    firsts = [
        ReduceFirst(sizes, wdown, cores[0], [(2, "l"), (3, "a"), (9, "w")], halves[0]),
        ReduceFirst(sizes, wdown, cores[1], [(4, "l"), (5, "a"), (2 * tiles - 1, "w")], halves[1]),
    ]
    seconds = [
        ReduceSecond(sizes, firsts[0], [(9, "l"), (10, "a"), (2 * tiles + 1, "w")]),
        ReduceSecond(sizes, firsts[1], [(2 * tiles - 1, "l"), (2 * tiles, "a"), (steps, "w")]),
    ]
    last_a = ReduceLast(sizes, seconds[0], [(2 * tiles + 1, "l"), (2 * tiles + 1, "a"), (steps, "w")])
    bup, wup, d_middle, d_attn, stat_two, bout, *moved = run(
        lambda *refs: mlp_kernel(*refs, tiles=tiles, deep=deep), steps,
        [
            once, pl.BlockSpec((step, width), turn(0, tiles, lambda i: (i, 0))),
            pl.BlockSpec((count, step), turn(0, tiles, lambda i: (0, i))), once,
            pl.BlockSpec((width, width), turn(2 * tiles, deep, lambda i: (0, i))), once, once, once, mod_once,
        ],
        [
            pl.BlockSpec((1, step), turn(0, tiles, lambda i: (0, i))),
            pl.BlockSpec((width, step), turn(tiles, tiles, lambda i: (0, i))),
            once, once, held((frames, 3, width)), held((1, width)),
        ],
        [
            like((1, hidden), f32), like((width, hidden), bf16), wide, acts, like((frames, 3, width), f32),
            like((1, width), f32),
        ],
        (d_branch, full_down, slope, act_two, full_up, middle, cotangent, attn, modulation),
        [pltpu.VMEM((count, hidden), bf16), acc], name="mlpb",
        moves=cores + firsts + seconds + [last_a], sizes=sizes, group=6,
    )
    down_b, wdown_low = moved[13:16], moved[16]
    wup = blocks(wup)
    halves = ((0, hidden // 2), (hidden // 2, hidden))
    quarters = 4
    quarter = width // quarters
    steps = quarters + pairs + 3
    cores = [ReduceCore(sizes, wup, [(0, "s"), (2 + i, "w")], h) for i, h in enumerate(halves)]
    firsts = [
        ReduceFirst(sizes, wup, cores[0], [(2, "l"), (3, "a"), (7, "w")], halves[0]),
        ReduceFirst(sizes, wup, cores[1], [(3, "l"), (4, "a"), (9, "w")], halves[1]),
    ]
    seconds = [
        ReduceSecond(sizes, firsts[0], [(7, "l"), (7, "a"), (10, "w")]),
        ReduceSecond(sizes, firsts[1], [(9, "l"), (9, "a"), (12, "w")]),
    ]
    last_b = ReduceLast(sizes, down_b, [(0, "l"), (1, "a"), (5, "w")])
    last_a = ReduceLast(sizes, seconds[0], [(10, "l"), (10, "a"), (steps, "w")])
    pair_b = pl.BlockSpec((count, LANE), turn(quarters, pairs, lambda i: (0, i)))
    table_once = held((count, LANE))
    wout, d_projected, bqkv, wqkv, *moved = run(
        lambda *refs: attention_back_kernel(*refs, frames=frames, lead=quarters, pairs=pairs), steps,
        [
            once, pl.BlockSpec((quarter, width), turn(0, quarters, lambda i: (i, 0))),
            pl.BlockSpec((count, quarter), turn(0, quarters, lambda i: (0, i))),
        ] + [pair_b] * 5 + [table_once] * 3 + [once],
        [
            pl.BlockSpec((quarter, width), turn(0, quarters, lambda i: (i, 0))),
            pl.BlockSpec((3, count, LANE), turn(quarters, pairs, lambda i: (0, 0, i))),
            pl.BlockSpec((1, 3, LANE), turn(quarters, pairs, lambda i: (i, 0, 0))),
            pl.BlockSpec((1, width, width), turn(quarters + pairs, 3, lambda i: (i, 0, 0))),
        ],
        [
            like((width, width), bf16), like((3, count, width), bf16), like((pairs, 3, LANE), f32),
            like((3, width, width), bf16),
        ],
        (d_attn, full_out, attended, query, key, value, attended, aug, see, cosine, sine, act_one),
        [pltpu.VMEM((count, width), bf16), pltpu.VMEM((3, count, width), bf16), pltpu.VMEM((count, LANE), f32)],
        name="attb", moves=[last_b] + cores + firsts + seconds + [last_a], sizes=sizes, group=7,
    )
    wdown_high, up_b, wup_low = moved[0], moved[14:17], moved[17]
    wdown_grad = jnp.concatenate([wdown_low, wdown_high], axis=1)
    wout, wqkv = blocks(wout), blocks(wqkv, 1)

    bqkv = jnp.transpose(bqkv, (1, 0, 2)).reshape(1, -1)
    shares = [b.reshape(ndev, -1) for b in (bqkv, bout, bup, bdown)]
    packed = jnp.concatenate(shares, axis=1)
    bias_len = packed.shape[1]
    packed = jnp.pad(packed, ((0, 0), (0, 8 * LANE - bias_len))).reshape(-1, LANE)
    packed = blocks(packed)
    mod_block = Held((6 * frames, width), bf16)
    d_mod = Gather(sizes, mod_block, ())
    sums, bias = [], Reduce(sizes, packed, ())
    for i in range(3):
        sums.append(Reduce(sizes, wqkv, [(0, "0"), (1 + i // 2, "1")] + [(2, "2")] * (i == 0), i))
    halves = ((0, width // 2), (width // 2, width))
    sums += [Reduce(sizes, wout, [(0, "0")], h) for h in halves]
    last_b = ReduceLast(sizes, up_b, [(0, "l"), (0, "a"), (3, "w")])

    def pack_modulation(ins, outs, scratch):
        one, two, gate = outs[1], ins[5], ins[6]
        parts = [one[:, 0, :], one[:, 1, :], two[:, 0, :], two[:, 1, :], two[:, 2, :], gate[...]]
        scratch[1][...] = jnp.concatenate(parts, axis=0).astype(bf16)

    def set_block(refs):
        mod_block.ref = refs[-1]
        input_back_kernel(*refs[:5], *refs[7:9], refs[9])

    q, k, v, oa, ob = sums
    token_grad, stat_one, *moved = run(
        lambda *refs: set_block(refs), 3,
        [stacked, by_cols(width, width), once, once, mod_once, held((frames, 3, width)), held((frames, width))],
        [once, held((frames, 2, width))],
        [acts, like((frames, 2, width), f32)],
        (d_projected, full_qkv, tokens, d_middle, modulation, stat_two, d_gate_two),
        [acc, pltpu.VMEM(mod_block.shape, bf16)], name="dact1",
        moves=[d_mod] + sums + [last_b, bias], sizes=sizes, group=8, axes="yxzc",
        script=[
            (oa, "1"), (ob, "1"), (bias, "0"), pack_modulation, (d_mod, "s0"), (k, "2"), (q, "3"), (bias, "1"),
            (v, "2"), (k, "3"), (d_mod, "n0"), (oa, "2"), (bias, "2"), (ob, "2"), (v, "3"), (q, "4"), (d_mod, "n1"),
            (bias, "3"), (oa, "3"), (ob, "3"), (k, "4"), (d_mod, "n2"), (bias, "4"), (v, "4"), (d_mod, "w3"),
            (oa, "4"), (ob, "4"),
        ],
    )
    d_mod, grad_q, grad_k, grad_v, wout_low, wout_high, wup_high, bias_sum = moved[:8]
    wout_grad = jnp.concatenate([wout_low, wout_high], axis=1)
    wup_grad = jnp.concatenate([wup_low, wup_high], axis=1)
    wqkv_grad = jnp.concatenate([grad_q, grad_k, grad_v], axis=1)
    d_mod = jnp.transpose(d_mod.reshape(ndev, 6, frames, width), (0, 2, 1, 3))
    d_mod = d_mod.reshape(ndev * frames, -1)
    bias_sum = bias_sum.reshape(-1)[:bias_len]
    bias_grads, at = [], 0
    for share in shares:
        bias_grads.append(bias_sum[at : at + share.shape[1]])
        at += share.shape[1]
    hot = (all_levels[:, None] == jnp.arange(noise_table.shape[1], dtype=jnp.int32)[None, :]).astype(bf16)
    embedded = dot(hot, noise_table, NT)
    cond = jax.nn.silu(embedded).astype(bf16)
    wmod_grad = dot(cond, d_mod, TN)
    mine = b_mod.shape[0]
    bmod_grad = jnp.sum(lax.dynamic_slice(d_mod, (0, me * mine), (d_mod.shape[0], mine)).astype(f32), axis=0)
    gate = jax.nn.sigmoid(embedded)
    d_embed = dot(d_mod, w_mod, NT) * gate * (1.0 + embedded * (1.0 - gate))
    table_grad = lax.dot_general(
        d_embed, hot.astype(f32), TN, precision=lax.Precision.HIGHEST, preferred_element_type=f32
    )
    return (
        block_out, token_grad, wmod_grad, bmod_grad, wqkv_grad, bias_grads[0], wout_grad, bias_grads[1],
        wup_grad, bias_grads[2], wdown_grad, bias_grads[3], table_grad,
    )


def solution(mesh):
    rows, vec = P(AXES, None), P(AXES)
    return jax.shard_map(
        per_device,
        mesh=mesh,
        in_specs=(rows, rows, rows, vec, vec) + (rows, vec) * 5 + (rows,),
        out_specs=(rows, rows) + (rows, vec) * 5 + (rows,),
        check_vma=False,
    )
```

profile of v0, /device:TPU:0, one launch (start us, length us, event | category | flops | bytes accessed | tf_op | source)
XLA Modules:
  0.0 429.2 jit_solution(16561818741286328099)
XLA Ops:
  0.6 0.8 select_reduce_fusion.5
  1.4 0.1 convert_reduce_fusion.1
  1.5 0.7 fusion.19
  2.2 0.2 select_reduce_fusion.4
  2.4 0.7 broadcast_compare_fusion
  3.1 0.1 select_reduce_fusion.3
  3.2 0.1 select_reduce_fusion
  3.3 1.5 pad.12.refs_0_
  4.8 0.1 broadcast_multiply_fusion.1
  4.9 0.7 tile.4
  5.6 0.1 tile.10
  5.7 3.4 concatenate.27
  9.1 0.6 pad_bitcast_fusion.refs_2_
  9.7 0.5 fusion.6
  10.2 1.5 select_convert_fusion.refs_6_.refs_8_
  11.7 0.9 compare_convert_fusion.refs_7_
  12.6 0.2 copy.50
  12.9 0.2 copy.46
  13.1 1.9 pad_maximum_fusion
  14.9 59.0 %head.1 = (f32[4,8,16,128]{3,2,1,0:T(8,128)}, bf16[2,2,4,2,32,3072]{5,4,3,2,1,0:T(8,128)(2,1)}, bf16[2,2,4,2,32,1024]{5,4,3,2,1,0:T(8,128)(2,1)}, bf16[2,2,4,2,32,4096]{5,4,3,2,1,0:T(8,128)(2,1)}, f32[8,3072]{1,0:T(8,128)}) custom-call(bf16[32,1024]{1,0:T(8,128)(2,1)} %pad.12.refs_0_, bf16[32,6144]{1,0:T(8,128)(2,1)} %refs_1_.1, ...), custom_call_target="tpu_custom_call" | custom-call | bytes 917504 | tf_op jit(solution)/shard_map/head/pallas_call | solution.py:965
  73.9 0.9 reshape.186
  74.8 0.1 copy.61
  74.9 0.1 reshape.187
  75.0 1.0 copy.60
  76.1 0.7 slice.56
  76.7 0.1 slice.54
  76.8 0.7 reshape.190.refs_3_
  77.5 0.1 fusion.21
  77.6 0.7 reshape.194.refs_2_
  78.3 0.1 add.71
  78.3 0.7 broadcast_add_fusion.refs_1_.refs_9_.refs_5_.refs_8_.refs_4_
  79.0 0.7 reshape.191.refs_10_
  79.7 0.1 reshape.204
  79.8 0.1 convert_element_type.77
  79.9 0.3 fusion.2
  80.2 96.1 %fwd.1 = (bf16[1024,1024]{1,0:T(8,128)(2,1)}, bf16[1024,1024]{1,0:T(8,128)(2,1)}, bf16[1024,1024]{1,0:T(8,128)(2,1)}, bf16[1024,1024]{1,0:T(8,128)(2,1)}, bf16[1...) custom-call(bf16[1024,1024]{1,0:T(8,128)(2,1)} %refs_2_.1, ...), custom_call_target="tpu_custom_call", output_to_operand_aliasing={{11}: (12, {}), {12}: (13, {})} | custom-call | bytes 24576000 | tf_op jit(solution)/shard_map/fwd/pallas_call | solution.py:965
  176.2 19.0 %down.1 = (bf16[1024,1024]{1,0:T(8,128)(2,1)}, bf16[1024,1024]{1,0:T(8,128)(2,1)}, f32[4,1024]{1,0:T(4,128)}, f32[1,1024]{1,0:T(1,128)}) custom-call(bf16[1024,4096]{1,0:T(8,128)(2,1)} %get-tuple-element.69.refs_0_, bf16[4096,1024]{1,0:T(8,128)(2,1)} %bitcast.57, f32[1,1024]{1,0:T(1,128)} %reshape.194.refs_2_, ...), custom_call_target="tpu_custom_call" | custom-call | bytes 46342144 | tf_op jit(solution)/shard_map/down/pallas_call | solution.py:965
  195.2 14.4 %wdown.1 = bf16[4096,1024]{1,0:T(8,128)(2,1)} custom-call(bf16[1024,4096]{1,0:T(8,128)(2,1)} %get-tuple-element.69.refs_0_, bf16[1024,1024]{1,0:T(8,128)(2,1)} %get-tuple-element.73.refs_1_.refs_0_), custom_call_target="tpu_custom_call" | custom-call | bytes 20971520 | tf_op jit(solution)/shard_map/wdown/pallas_call | solution.py:965
  209.6 65.1 %mlpb.1 = (f32[1,4096]{1,0:T(1,128)}, bf16[1024,4096]{1,0:T(8,128)(2,1)}, f32[1024,1024]{1,0:T(8,128)}, bf16[1024,1024]{1,0:T(8,128)(2,1)}, f32[4,3,1024]{2,1,0:...) custom-call(bf16[1024,1024]{1,0:T(8,128)(2,1)} %get-tuple-element.73, ...), custom_call_target="tpu_custom_call" | custom-call | bytes 75694080 | tf_op jit(solution)/shard_map/mlpb/pallas_call | solution.py:965
  274.7 71.3 %attb.1 = (bf16[1024,1024]{1,0:T(8,128)(2,1)}, bf16[3,1024,1024]{2,1,0:T(8,128)(2,1)}, f32[8,3,128]{2,1,0:T(4,128)}, bf16[3,1024,1024]{2,1,0:T(8,128)(2,1)}, f32...) custom-call(bf16[1024,1024]{1,0:T(8,128)(2,1)} %get-tuple-element.78, ...), custom_call_target="tpu_custom_call" | custom-call | bytes 40370176 | tf_op jit(solution)/shard_map/attb/pallas_call | solution.py:965
  346.0 0.5 broadcast.176
  346.6 0.7 reduce.6
  347.2 0.7 reduce.7
  347.9 0.1 reshape.201
  348.1 0.7 copy.53
  348.8 0.1 reshape_reshape.6
  348.9 0.1 fusion.5
  348.9 0.7 copy.56
  349.6 63.3 %dact1.1 = (bf16[1024,1024]{1,0:T(8,128)(2,1)}, f32[4,2,1024]{2,1,0:T(2,128)}, bf16[2,2,4,2,24,1024]{5,4,3,2,1,0:T(8,128)(2,1)}, f32[32,1024]{1,0:T(8,128)}, f32...) custom-call(bf16[3,1024,1024]{2,1,0:T(8,128)(2,1)} %get-tuple-elemen, ...), custom_call_target="tpu_custom_call" | custom-call | bytes 38076416 | tf_op jit(solution)/shard_map/dact1/pallas_call | solution.py:965
  413.0 1.3 slice.48
  414.3 1.2 slice_bitcast_fusion
  415.5 1.3 fusion.22
  416.8 1.5 pad_maximum_fusion.6
  418.4 1.8 pad_maximum_fusion.2
  420.1 0.8 pad_maximum_fusion.3
  421.0 0.8 pad_maximum_fusion.4
  421.7 0.6 reshape.205
  422.4 0.7 copy.54
  423.1 1.0 copy.57
  424.1 0.7 convert_reduce_fusion
  424.8 0.6 fusion
  425.4 1.2 fusion.8
  426.7 1.0 fusion.1
  427.7 1.3 copy.65
  (39 shorter events, 0.2 us)
Async XLA Ops:
  14.9 65.0 %copy-start.9 = (bf16[32,1000]{1,0:T(8,128)(2,1)S(1)}, bf16[32,1000]{1,0:T(8,128)(2,1)}, u32[]{:S(2)}) copy-start(bf16[32,1000]{1,0:T(8,128)(2,1)} %param.31) | copy-start | bytes 192004
  274.7 71.9 %copy-start.11 = (f32[1,1024]{1,0:T(1,128)S(1)}, f32[1,1024]{1,0:T(1,128)}, u32[]{:S(2)}) copy-start(f32[1,1024]{1,0:T(1,128)} %get-tuple-element.102) | copy-start | bytes 12292
  274.7 72.5 %copy-start.12 = (f32[1,1024]{1,0:T(1,128)S(1)}, f32[1,1024]{1,0:T(1,128)}, u32[]{:S(2)}) copy-start(f32[1,1024]{1,0:T(1,128)} %get-tuple-element.100) | copy-start | bytes 12292
  274.7 74.1 %copy-start.10 = (f32[1,4096]{1,0:T(1,128)S(1)}, f32[1,4096]{1,0:T(1,128)}, u32[]{:S(2)}) copy-start(f32[1,4096]{1,0:T(1,128)} %get-tuple-element.101) | copy-start | bytes 49156
  349.6 68.7 %copy-start.5 = (f32[32,2048]{1,0:T(8,128)S(1)}, f32[32,2048]{1,0:T(8,128)}, u32[]{:S(2)}) copy-start(f32[32,2048]{1,0:T(8,128)} %get-tuple-element.111) | copy-start | bytes 786436
  349.6 70.5 %copy-start.3 = (f32[128,512]{1,0:T(8,128)S(1)}, f32[128,512]{1,0:T(8,128)}, u32[]{:S(2)}) copy-start(f32[128,512]{1,0:T(8,128)} %get-tuple-element.113) | copy-start | bytes 786436
  349.6 70.5 %copy-start.4 = (f32[128,512]{1,0:T(8,128)S(1)}, f32[128,512]{1,0:T(8,128)}, u32[]{:S(2)}) copy-start(f32[128,512]{1,0:T(8,128)} %get-tuple-element.114) | copy-start | bytes 786436
  412.9 8.0 %copy-start.6 = (f32[32,1024]{1,0:T(8,128)S(1)}, f32[32,1024]{1,0:T(8,128)}, u32[]{:S(2)}) copy-start(f32[32,1024]{1,0:T(8,128)} %get-tuple-element.105) | copy-start | bytes 393220
  412.9 8.0 %copy-start.7 = (f32[32,1024]{1,0:T(8,128)S(1)}, f32[32,1024]{1,0:T(8,128)}, u32[]{:S(2)}) copy-start(f32[32,1024]{1,0:T(8,128)} %get-tuple-element.106) | copy-start | bytes 393220
  413.0 8.0 %copy-start.8 = (f32[32,1024]{1,0:T(8,128)S(1)}, f32[32,1024]{1,0:T(8,128)}, u32[]{:S(2)}) copy-start(f32[32,1024]{1,0:T(8,128)} %get-tuple-element.107) | copy-start | bytes 393220
  413.0 8.8 %copy-start.1 = (bf16[2,2,4,2,24,1024]{5,4,3,2,1,0:T(8,128)(2,1)S(1)}, bf16[2,2,4,2,24,1024]{5,4,3,2,1,0:T(8,128)(2,1)}, u32[]{:S(2)}) copy-start(bf16[2,2,4,2,24,1024]{5,4,3,2,1,0:T(8,128)(2,1)} %get-tuple-element.104) | copy-start | bytes 4718596
  423.1 1.7 copy-start.2
  424.8 2.9 copy-start
where the time goes:
time: 435 us; the launch traced here: 429 us
  Pallas kernels  388 us (89%)
  local copies, waits for them, and re-layouts  21.6 us (5%)
  other arithmetic  15.2 us (3%)
    pallas_call x7, Pallas kernels, run(): pl.pallas_call(body, grid=(grid,), in_specs=all_specs, out_specs=all_out_...  388 us

commit v1 on v0

--- a/solution.py
+++ b/solution.py
@@ -205,10 +205,24 @@
 
 def mlp_kernel(
     dbr_ref, wdown_ref, slope_ref, act_ref, wup_ref, mid_ref, cot_ref, attn_ref, mod_ref,
-    bup_ref, out_ref, dmid_ref, datt_ref, stat_ref, sum_ref, dh_ref, acc_ref, *, tiles, deep,
+    bup_ref, out_ref, dmid_ref, datt_ref, stat_ref, sum_ref, dh_ref, acc_ref, mid_all, cot_all, attn_all, sems,
+    *, tiles, deep,
 ):
     step = pl.program_id(0)
     size, wide = dh_ref.shape[1] // tiles, dh_ref.shape[1] // deep
+    late = [
+        (mid_ref, mid_all, sems.at[0]), (cot_ref, cot_all, sems.at[1]), (attn_ref, attn_all, sems.at[2])
+    ]
+
+    @pl.when(step == 1)
+    def _():
+        for item in late:
+            pltpu.make_async_copy(*item).start()
+
+    @pl.when(step == 2 * tiles)
+    def _():
+        for item in late:
+            pltpu.make_async_copy(*item).wait()
 
     @pl.when(step < tiles)
     def _():
@@ -221,7 +235,7 @@
     @pl.when(step >= 2 * tiles)
     def _():
         mlp_back_kernel(
-            at_columns(dh_ref, step - 2 * tiles, wide), wup_ref, mid_ref, cot_ref, attn_ref, mod_ref,
+            at_columns(dh_ref, step - 2 * tiles, wide), wup_ref, mid_all, cot_all, attn_all, mod_ref,
             dmid_ref, datt_ref, stat_ref, sum_ref, acc_ref, step - 2 * tiles, deep - 1,
         )
 
@@ -666,14 +680,14 @@
 
 
 class Reduce(Move):
-    def __init__(self, sizes, array, actions, part=None):
-        self.actions, self.part = actions, part
+    def __init__(self, sizes, array, actions, part=None, into=None):
+        self.actions, self.part, self.into = actions, part, into
         ny, nx, nz = sizes
         half, rest = nz // 2, nz - nz // 2
         block, kind = block_of(array, part), array.dtype
         self.held = array if isinstance(array, Held) else None
         self.ins, self.in_specs = ([], []) if self.held else ([array], [ANY])
-        self.outs, self.out_specs = [like(block, f32)], [VMEM]
+        self.outs, self.out_specs = ([like(block, f32)], [VMEM]) if into is None else ([], [])
         shapes = [
             (ny, nx, nz), (ny, nx, nz), (ny - 1, nx, half), (nx - 1, ny, rest), (nx - 1, half), (ny - 1, rest), (nz - 1,)
         ]
@@ -728,7 +742,11 @@
             value = acc[y, x, z].astype(f32)
             for k in range(p.nz - 1):
                 value = value + last[k].astype(f32)
-            self.out_refs[0][...] = value
+            if self.into is None:
+                self.out_refs[0][...] = value
+            else:
+                held, start = self.into
+                held.ref[:, start : start + value.shape[1]] = value
             for at in range(4):
                 self.drain(leaving(at))
 
@@ -1043,7 +1061,7 @@
     packed = jnp.concatenate([mine_at.astype(f32)] + [b.astype(f32) for b in biases])
     packed = jnp.pad(packed, (0, 16 * LANE - packed.shape[0])).reshape(16, LANE)
     table_pad = jnp.pad(noise_table, ((0, 0), (0, -noise_table.shape[1] % LANE)))
-    part = Held(lead + (2 * frames, w_mod.shape[1] // 2), bf16)
+    part = Held(lead + (2 * frames, w_mod.shape[1] // 2), f32)
     small = Spread(sizes, packed)
     qkv_w = Gather(sizes, w_qkv, ())
     out_w, up_w = Gather(sizes, w_out, ()), Gather(sizes, w_up, ())
@@ -1058,7 +1076,7 @@
 
     head = run(
         None, 1, [VMEM] * 2, [], [], [table_pad, w_mod],
-        [pltpu.VMEM(part.shape, bf16), pltpu.VMEM(small.outs[0].shape, f32), DMA((1,))], name="head",
+        [pltpu.VMEM(part.shape, f32), pltpu.VMEM(small.outs[0].shape, f32), DMA((1,))], name="head",
         moves=[small, qkv_w, out_w, up_w, mod_sum], sizes=sizes, group=1, axes="df",
         script=[
             (small, "0"), (qkv_w, "s0a"), (qkv_w, "s0b"), (out_w, "s0"), (small, "1"), (small, "2"), add_modulation,
@@ -1158,22 +1176,18 @@
     mod_once = held((frames, 6, width))
     halves = ((0, width // 2), (width // 2, width))
     steps = 2 * tiles + deep
-    cores = [ReduceCore(sizes, wdown, [(0, "s"), (2 + 2 * i, "w")], h) for i, h in enumerate(halves)]
-    firsts = [
-        ReduceFirst(sizes, wdown, cores[0], [(2, "l"), (3, "a"), (9, "w")], halves[0]),
-        ReduceFirst(sizes, wdown, cores[1], [(4, "l"), (5, "a"), (2 * tiles - 1, "w")], halves[1]),
-    ]
-    seconds = [
-        ReduceSecond(sizes, firsts[0], [(9, "l"), (10, "a"), (2 * tiles + 1, "w")]),
-        ReduceSecond(sizes, firsts[1], [(2 * tiles - 1, "l"), (2 * tiles, "a"), (steps, "w")]),
-    ]
-    last_a = ReduceLast(sizes, seconds[0], [(2 * tiles + 1, "l"), (2 * tiles + 1, "a"), (steps, "w")])
+    sum_a = Reduce(
+        sizes, wdown, [(0, "0"), (2, "1"), (tiles, "2"), (2 * tiles, "3"), (steps, "4")], halves[0]
+    )
+    core = ReduceCore(sizes, wdown, [(0, "s"), (3, "w")], halves[1])
+    first = ReduceFirst(sizes, wdown, core, [(3, "l"), (4, "a"), (2 * tiles - 1, "w")], halves[1])
+    second = ReduceSecond(sizes, first, [(2 * tiles - 1, "l"), (2 * tiles, "a"), (steps, "w")])
     bup, wup, d_middle, d_attn, stat_two, bout, *moved = run(
         lambda *refs: mlp_kernel(*refs, tiles=tiles, deep=deep), steps,
         [
             once, pl.BlockSpec((step, width), turn(0, tiles, lambda i: (i, 0))),
             pl.BlockSpec((count, step), turn(0, tiles, lambda i: (0, i))), once,
-            pl.BlockSpec((width, width), turn(2 * tiles, deep, lambda i: (0, i))), once, once, once, mod_once,
+            pl.BlockSpec((width, width), turn(2 * tiles, deep, lambda i: (0, i))), ANY, ANY, ANY, mod_once,
         ],
         [
             pl.BlockSpec((1, step), turn(0, tiles, lambda i: (0, i))),
@@ -1185,26 +1199,23 @@
             like((1, width), f32),
         ],
         (d_branch, full_down, slope, act_two, full_up, middle, cotangent, attn, modulation),
-        [pltpu.VMEM((count, hidden), bf16), acc], name="mlpb",
-        moves=cores + firsts + seconds + [last_a], sizes=sizes, group=6,
-    )
-    down_b, wdown_low = moved[13:16], moved[16]
+        [
+            pltpu.VMEM((count, hidden), bf16), acc, acc, pltpu.VMEM((count, width), bf16),
+            pltpu.VMEM((count, width), bf16), DMA((3,)),
+        ],
+        name="mlpb", moves=[sum_a, core, first, second], sizes=sizes, group=6,
+    )
+    wdown_low, down_b = moved[0], moved[6:9]
     wup = blocks(wup)
     halves = ((0, hidden // 2), (hidden // 2, hidden))
     quarters = 4
     quarter = width // quarters
     steps = quarters + pairs + 3
-    cores = [ReduceCore(sizes, wup, [(0, "s"), (2 + i, "w")], h) for i, h in enumerate(halves)]
-    firsts = [
-        ReduceFirst(sizes, wup, cores[0], [(2, "l"), (3, "a"), (7, "w")], halves[0]),
-        ReduceFirst(sizes, wup, cores[1], [(3, "l"), (4, "a"), (9, "w")], halves[1]),
-    ]
-    seconds = [
-        ReduceSecond(sizes, firsts[0], [(7, "l"), (7, "a"), (10, "w")]),
-        ReduceSecond(sizes, firsts[1], [(9, "l"), (9, "a"), (12, "w")]),
-    ]
+    sum_a = Reduce(sizes, wup, [(0, "0"), (2, "1"), (6, "2"), (9, "3"), (steps, "4")], halves[0])
+    core = ReduceCore(sizes, wup, [(0, "s"), (3, "w")], halves[1])
+    first = ReduceFirst(sizes, wup, core, [(3, "l"), (4, "a"), (9, "w")], halves[1])
+    second = ReduceSecond(sizes, first, [(9, "l"), (9, "a"), (12, "w")])
     last_b = ReduceLast(sizes, down_b, [(0, "l"), (1, "a"), (5, "w")])
-    last_a = ReduceLast(sizes, seconds[0], [(10, "l"), (10, "a"), (steps, "w")])
     pair_b = pl.BlockSpec((count, LANE), turn(quarters, pairs, lambda i: (0, i)))
     table_once = held((count, LANE))
     wout, d_projected, bqkv, wqkv, *moved = run(
@@ -1225,9 +1236,9 @@
         ],
         (d_attn, full_out, attended, query, key, value, attended, aug, see, cosine, sine, act_one),
         [pltpu.VMEM((count, width), bf16), pltpu.VMEM((3, count, width), bf16), pltpu.VMEM((count, LANE), f32)],
-        name="attb", moves=[last_b] + cores + firsts + seconds + [last_a], sizes=sizes, group=7,
-    )
-    wdown_high, up_b, wup_low = moved[0], moved[14:17], moved[17]
+        name="attb", moves=[last_b, sum_a, core, first, second], sizes=sizes, group=7,
+    )
+    wdown_high, wup_low, up_b = moved[0], moved[1], moved[7:10]
     wdown_grad = jnp.concatenate([wdown_low, wdown_high], axis=1)
     wout, wqkv = blocks(wout), blocks(wqkv, 1)
 
@@ -1239,42 +1250,41 @@
     packed = blocks(packed)
     mod_block = Held((6 * frames, width), bf16)
     d_mod = Gather(sizes, mod_block, ())
-    sums, bias = [], Reduce(sizes, packed, ())
-    for i in range(3):
-        sums.append(Reduce(sizes, wqkv, [(0, "0"), (1 + i // 2, "1")] + [(2, "2")] * (i == 0), i))
+    bias = Reduce(sizes, packed, ())
+    qkv_out, out_out = Held((width // ndev, 3 * width), f32), Held((width // ndev, width), f32)
+    marks = ([(0, "0"), (0, "1"), (1, "2"), (2, "3")], [(0, "0"), (0, "1"), (2, "2")], [(0, "0"), (1, "1")])
+    q, k, v = [Reduce(sizes, wqkv, marks[i], i, (qkv_out, i * width)) for i in range(3)]
     halves = ((0, width // 2), (width // 2, width))
-    sums += [Reduce(sizes, wout, [(0, "0")], h) for h in halves]
+    oa = Reduce(sizes, wout, [(0, "0"), (2, "1")], halves[0], (out_out, 0))
+    ob = Reduce(sizes, wout, [(0, "0")], halves[1], (out_out, width // 2))
     last_b = ReduceLast(sizes, up_b, [(0, "l"), (0, "a"), (3, "w")])
 
     def pack_modulation(ins, outs, scratch):
         one, two, gate = outs[1], ins[5], ins[6]
         parts = [one[:, 0, :], one[:, 1, :], two[:, 0, :], two[:, 1, :], two[:, 2, :], gate[...]]
+        mod_block.ref = scratch[1]
+        qkv_out.ref, out_out.ref = outs[2:]
         scratch[1][...] = jnp.concatenate(parts, axis=0).astype(bf16)
 
     def set_block(refs):
-        mod_block.ref = refs[-1]
-        input_back_kernel(*refs[:5], *refs[7:9], refs[9])
-
-    q, k, v, oa, ob = sums
-    token_grad, stat_one, *moved = run(
+        input_back_kernel(*refs[:5], *refs[7:9], refs[11])
+
+    token_grad, stat_one, wqkv_grad, wout_grad, *moved = run(
         lambda *refs: set_block(refs), 3,
         [stacked, by_cols(width, width), once, once, mod_once, held((frames, 3, width)), held((frames, width))],
-        [once, held((frames, 2, width))],
-        [acts, like((frames, 2, width), f32)],
+        [once, held((frames, 2, width)), VMEM, VMEM],
+        [acts, like((frames, 2, width), f32), like(qkv_out.shape, f32), like(out_out.shape, f32)],
         (d_projected, full_qkv, tokens, d_middle, modulation, stat_two, d_gate_two),
         [acc, pltpu.VMEM(mod_block.shape, bf16)], name="dact1",
-        moves=[d_mod] + sums + [last_b, bias], sizes=sizes, group=8, axes="yxzc",
+        moves=[d_mod, q, k, v, oa, ob, last_b, bias], sizes=sizes, group=8,
         script=[
-            (oa, "1"), (ob, "1"), (bias, "0"), pack_modulation, (d_mod, "s0"), (k, "2"), (q, "3"), (bias, "1"),
-            (v, "2"), (k, "3"), (d_mod, "n0"), (oa, "2"), (bias, "2"), (ob, "2"), (v, "3"), (q, "4"), (d_mod, "n1"),
-            (bias, "3"), (oa, "3"), (ob, "3"), (k, "4"), (d_mod, "n2"), (bias, "4"), (v, "4"), (d_mod, "w3"),
-            (oa, "4"), (ob, "4"),
+            (bias, "0"), pack_modulation, (d_mod, "s0"), (v, "2"), (k, "3"), (ob, "1"), (bias, "1"), (oa, "2"), (v, "3"),
+            (d_mod, "n0"), (ob, "2"), (bias, "2"), (oa, "3"), (ob, "3"), (d_mod, "n1"), (bias, "3"), (q, "4"), (k, "4"),
+            (d_mod, "n2"), (bias, "4"), (v, "4"), (d_mod, "w3"), (oa, "4"), (ob, "4"),
         ],
     )
-    d_mod, grad_q, grad_k, grad_v, wout_low, wout_high, wup_high, bias_sum = moved[:8]
-    wout_grad = jnp.concatenate([wout_low, wout_high], axis=1)
+    d_mod, wup_high, bias_sum = moved
     wup_grad = jnp.concatenate([wup_low, wup_high], axis=1)
-    wqkv_grad = jnp.concatenate([grad_q, grad_k, grad_v], axis=1)
     d_mod = jnp.transpose(d_mod.reshape(ndev, 6, frames, width), (0, 2, 1, 3))
     d_mod = d_mod.reshape(ndev * frames, -1)
     bias_sum = bias_sum.reshape(-1)[:bias_len]

time: 435 us -> 428 us (0.984)
  Pallas kernels: 388 us -> 382 us
    pallas_call x7, Pallas kernels: 388 us -> 382 us  [run(): pl.pallas_call(body, grid=(grid,), in_specs=all_specs, out_specs=all_out_...]
where the time goes in v1:
time: 428 us; the launch traced here: 422 us
  Pallas kernels  382 us (89%)
  local copies, waits for them, and re-layouts  23 us (5%)
  other arithmetic  12.9 us (3%)
    pallas_call x7, Pallas kernels, run(): pl.pallas_call(body, grid=(grid,), in_specs=all_specs, out_specs=all_out_...  382 us

profile of v1, /device:TPU:0, one launch (start us, length us, event | category | flops | bytes accessed | tf_op | source)
XLA Modules:
  0.0 422.0 jit_solution(16752005575486191497)
XLA Ops:
  0.6 0.8 select_reduce_fusion.5
  1.4 0.1 convert_reduce_fusion.1
  1.5 0.7 fusion.19
  2.2 0.2 select_reduce_fusion.4
  2.4 0.7 broadcast_compare_fusion
  3.1 0.1 select_reduce_fusion.3
  3.2 0.1 select_reduce_fusion
  3.3 1.5 pad.12.refs_0_
  4.8 0.1 broadcast_multiply_fusion.1
  4.9 0.7 tile.4
  5.6 0.1 tile.10
  5.7 3.4 concatenate.21
  9.1 0.6 pad_bitcast_fusion.refs_2_
  9.7 0.5 fusion.6
  10.2 1.5 select_convert_fusion.refs_6_.refs_8_
  11.7 0.9 compare_convert_fusion.refs_7_
  12.6 0.2 copy.50
  12.9 0.2 copy.46
  13.1 1.9 pad_maximum_fusion
  14.9 65.3 %head.1 = (f32[4,8,16,128]{3,2,1,0:T(8,128)}, bf16[2,2,4,2,32,3072]{5,4,3,2,1,0:T(8,128)(2,1)}, bf16[2,2,4,2,32,1024]{5,4,3,2,1,0:T(8,128)(2,1)}, bf16[2,2,4,2,32,4096]{5,4,3,2,1,0:T(8,128)(2,1)}, f32[8,3072]{1,0:T(8,128)}) custom-call(bf16[32,1024]{1,0:T(8,128)(2,1)} %pad.12.refs_0_, bf16[32,6144]{1,0:T(8,128)(2,1)} %refs_1_.1, ...), custom_call_target="tpu_custom_call" | custom-call | bytes 917504 | tf_op jit(solution)/shard_map/head/pallas_call | solution.py:983
  80.3 0.9 reshape.186
  81.2 0.1 copy.61
  81.3 0.1 reshape.187
  81.4 1.0 copy.60
  82.4 0.7 slice.56
  83.1 0.1 slice.54
  83.2 0.7 reshape.190.refs_3_
  83.9 0.1 fusion.21
  84.0 0.7 reshape.194.refs_2_
  84.6 0.1 add.71
  84.7 0.7 broadcast_add_fusion.refs_1_.refs_9_.refs_5_.refs_8_.refs_4_
  85.4 0.7 reshape.191.refs_10_
  86.1 0.1 reshape.204
  86.2 0.1 convert_element_type.77
  86.3 0.3 fusion.2
  86.5 95.9 %fwd.1 = (bf16[1024,1024]{1,0:T(8,128)(2,1)}, bf16[1024,1024]{1,0:T(8,128)(2,1)}, bf16[1024,1024]{1,0:T(8,128)(2,1)}, bf16[1024,1024]{1,0:T(8,128)(2,1)}, bf16[1...) custom-call(bf16[1024,1024]{1,0:T(8,128)(2,1)} %refs_2_.1, ...), custom_call_target="tpu_custom_call", output_to_operand_aliasing={{11}: (12, {}), {12}: (13, {})} | custom-call | bytes 24576000 | tf_op jit(solution)/shard_map/fwd/pallas_call | solution.py:983
  182.4 19.0 %down.1 = (bf16[1024,1024]{1,0:T(8,128)(2,1)}, bf16[1024,1024]{1,0:T(8,128)(2,1)}, f32[4,1024]{1,0:T(4,128)}, f32[1,1024]{1,0:T(1,128)}) custom-call(bf16[1024,4096]{1,0:T(8,128)(2,1)} %get-tuple-element.66.refs_0_, bf16[4096,1024]{1,0:T(8,128)(2,1)} %bitcast.55, f32[1,1024]{1,0:T(1,128)} %reshape.194.refs_2_, ...), custom_call_target="tpu_custom_call" | custom-call | bytes 46342144 | tf_op jit(solution)/shard_map/down/pallas_call | solution.py:983
  201.4 14.4 %wdown.1 = bf16[4096,1024]{1,0:T(8,128)(2,1)} custom-call(bf16[1024,4096]{1,0:T(8,128)(2,1)} %get-tuple-element.66.refs_0_, bf16[1024,1024]{1,0:T(8,128)(2,1)} %get-tuple-element.70.refs_1_.refs_0_), custom_call_target="tpu_custom_call" | custom-call | bytes 20971520 | tf_op jit(solution)/shard_map/wdown/pallas_call | solution.py:983
  215.8 61.6 %mlpb.1 = (f32[1,4096]{1,0:T(1,128)}, bf16[1024,4096]{1,0:T(8,128)(2,1)}, f32[1024,1024]{1,0:T(8,128)}, bf16[1024,1024]{1,0:T(8,128)(2,1)}, f32[4,3,1024]{2,1,0:...) custom-call(bf16[1024,1024]{1,0:T(8,128)(2,1)} %get-tuple-element.70, ...), custom_call_target="tpu_custom_call" | custom-call | bytes 75694080 | tf_op jit(solution)/shard_map/mlpb/pallas_call | solution.py:983
  277.4 65.9 %attb.1 = (bf16[1024,1024]{1,0:T(8,128)(2,1)}, bf16[3,1024,1024]{2,1,0:T(8,128)(2,1)}, f32[8,3,128]{2,1,0:T(4,128)}, bf16[3,1024,1024]{2,1,0:T(8,128)(2,1)}, f32...) custom-call(bf16[1024,1024]{1,0:T(8,128)(2,1)} %get-tuple-element.75, ...), custom_call_target="tpu_custom_call" | custom-call | bytes 40370176 | tf_op jit(solution)/shard_map/attb/pallas_call | solution.py:983
  343.3 0.5 broadcast.176
  343.8 0.7 reduce.6
  344.5 0.7 reduce.7
  345.1 0.1 reshape.201
  345.3 0.7 copy.53
  346.0 0.1 reshape_reshape.6
  346.1 0.1 fusion.5
  346.2 0.7 copy.56
  346.8 59.8 %dact1.1 = (bf16[1024,1024]{1,0:T(8,128)(2,1)}, f32[4,2,1024]{2,1,0:T(2,128)}, f32[32,3072]{1,0:T(8,128)}, f32[32,1024]{1,0:T(8,128)}, bf16[2,2,4,2,24,1024]{5,4...) custom-call(bf16[3,1024,1024]{2,1,0:T(8,128)(2,1)} %get-tuple-element.87.refs_0_, ...), custom_call_target="tpu_custom_call" | custom-call | bytes 38076416 | tf_op jit(solution)/shard_map/dact1/pallas_call | solution.py:983
  406.6 1.3 slice.48
  407.9 1.2 slice_bitcast_fusion
  409.1 1.3 fusion.22
  410.5 1.8 pad_maximum_fusion.2
  412.3 0.8 pad_maximum_fusion.3
  413.1 0.6 reshape.205
  413.7 0.7 copy.54
  414.4 1.0 copy.57
  415.5 0.7 convert_reduce_fusion
  416.2 0.6 fusion
  416.8 1.2 fusion.8
  418.0 1.0 fusion.1
  419.0 1.3 copy.67
  420.4 0.7 copy.68
  421.1 0.7 copy.69
  (37 shorter events, 0.2 us)
Async XLA Ops:
  14.9 71.3 %copy-start.8 = (bf16[32,1000]{1,0:T(8,128)(2,1)S(1)}, bf16[32,1000]{1,0:T(8,128)(2,1)}, u32[]{:S(2)}) copy-start(bf16[32,1000]{1,0:T(8,128)(2,1)} %param.31) | copy-start | bytes 192004
  277.4 66.4 %copy-start.10 = (f32[1,1024]{1,0:T(1,128)S(1)}, f32[1,1024]{1,0:T(1,128)}, u32[]{:S(2)}) copy-start(f32[1,1024]{1,0:T(1,128)} %get-tuple-element.99) | copy-start | bytes 12292
  277.4 67.1 %copy-start.11 = (f32[1,1024]{1,0:T(1,128)S(1)}, f32[1,1024]{1,0:T(1,128)}, u32[]{:S(2)}) copy-start(f32[1,1024]{1,0:T(1,128)} %get-tuple-element.97) | copy-start | bytes 12292
  277.4 68.7 %copy-start.9 = (f32[1,4096]{1,0:T(1,128)S(1)}, f32[1,4096]{1,0:T(1,128)}, u32[]{:S(2)}) copy-start(f32[1,4096]{1,0:T(1,128)} %get-tuple-element.98) | copy-start | bytes 49156
  346.8 63.6 %copy-start.6 = (f32[32,2048]{1,0:T(8,128)S(1)}, f32[32,2048]{1,0:T(8,128)}, u32[]{:S(2)}) copy-start(f32[32,2048]{1,0:T(8,128)} %get-tuple-element.105) | copy-start | bytes 786436
  346.8 65.4 %copy-start.4 = (f32[128,512]{1,0:T(8,128)S(1)}, f32[128,512]{1,0:T(8,128)}, u32[]{:S(2)}) copy-start(f32[128,512]{1,0:T(8,128)} %get-tuple-element.107) | copy-start | bytes 786436
  346.8 65.4 %copy-start.5 = (f32[128,512]{1,0:T(8,128)S(1)}, f32[128,512]{1,0:T(8,128)}, u32[]{:S(2)}) copy-start(f32[128,512]{1,0:T(8,128)} %get-tuple-element.108) | copy-start | bytes 786436
  406.6 6.5 %copy-start.1 = (bf16[2,2,4,2,24,1024]{5,4,3,2,1,0:T(8,128)(2,1)S(1)}, bf16[2,2,4,2,24,1024]{5,4,3,2,1,0:T(8,128)(2,1)}, u32[]{:S(2)}) copy-start(bf16[2,2,4,2,24,1024]{5,4,3,2,1,0:T(8,128)(2,1)} %get-tuple-element.101) | copy-start | bytes 4718596
  414.4 1.7 copy-start.2
  416.2 2.9 copy-start
  419.0 1.3 copy-start.3
  419.0 2.1 copy-start.7

commit v2 on v1

--- a/solution.py
+++ b/solution.py
@@ -1060,7 +1060,6 @@
     mine_at = jnp.where(spots // (2 * frames) == me, jnp.tile(levels, spots.shape[0] // frames), 0)
     packed = jnp.concatenate([mine_at.astype(f32)] + [b.astype(f32) for b in biases])
     packed = jnp.pad(packed, (0, 16 * LANE - packed.shape[0])).reshape(16, LANE)
-    table_pad = jnp.pad(noise_table, ((0, 0), (0, -noise_table.shape[1] % LANE)))
     part = Held(lead + (2 * frames, w_mod.shape[1] // 2), f32)
     small = Spread(sizes, packed)
     qkv_w = Gather(sizes, w_qkv, ())
@@ -1075,7 +1074,7 @@
         modulation_kernel(None, ins[0], ins[1], scratch[0], scratch[1], frames)
 
     head = run(
-        None, 1, [VMEM] * 2, [], [], [table_pad, w_mod],
+        None, 1, [VMEM] * 2, [], [], [noise_table, w_mod],
         [pltpu.VMEM(part.shape, f32), pltpu.VMEM(small.outs[0].shape, f32), DMA((1,))], name="head",
         moves=[small, qkv_w, out_w, up_w, mod_sum], sizes=sizes, group=1, axes="df",
         script=[
@@ -1123,12 +1122,12 @@
     pair_one = pl.BlockSpec((count, LANE), turn(frames, pairs, lambda i: (0, i)))
     cols_one = pl.BlockSpec((count, step), turn(m2, tiles, lambda i: (0, i)))
     move_out = Gather(
-        sizes, out_w, [(0, "s1"), (4, "n1"), (8, "n2"), (9, "w3"), (9, "l"), (m1, "d")], True, load=True
+        sizes, out_w, [(0, "s1"), (3, "n1"), (8, "n2"), (9, "w3"), (9, "l"), (m1, "d")], True, load=True
     )
     move_up = Gather(
         sizes, up_w,
         [
-            (0, "s1a"), (0, "s0b"), (2, "n1a"), (5, "n0b"), (6, "n2a"), (7, "w3a"), (7, "la"), (9, "n1b"), (m2, "da"),
+            (0, "s1a"), (0, "s0b"), (2, "n1a"), (5, "n0b"), (7, "n2a"), (8, "w3a"), (8, "la"), (9, "n1b"), (m2, "da"),
             (m2 + 1, "n2b"), (m2 + 2, "w3b"), (m2 + 2, "lb"), (m2 + tiles // 2, "db"),
         ], True, w_up, True,
     )
@@ -1177,11 +1176,11 @@
     halves = ((0, width // 2), (width // 2, width))
     steps = 2 * tiles + deep
     sum_a = Reduce(
-        sizes, wdown, [(0, "0"), (2, "1"), (tiles, "2"), (2 * tiles, "3"), (steps, "4")], halves[0]
+        sizes, wdown, [(0, "0"), (2, "1"), (tiles + 1, "2"), (2 * tiles + 2, "3"), (steps, "4")], halves[0]
     )
     core = ReduceCore(sizes, wdown, [(0, "s"), (3, "w")], halves[1])
-    first = ReduceFirst(sizes, wdown, core, [(3, "l"), (4, "a"), (2 * tiles - 1, "w")], halves[1])
-    second = ReduceSecond(sizes, first, [(2 * tiles - 1, "l"), (2 * tiles, "a"), (steps, "w")])
+    first = ReduceFirst(sizes, wdown, core, [(3, "l"), (4, "a"), (2 * tiles, "w")], halves[1])
+    second = ReduceSecond(sizes, first, [(2 * tiles, "l"), (2 * tiles + 1, "a"), (steps, "w")])
     bup, wup, d_middle, d_attn, stat_two, bout, *moved = run(
         lambda *refs: mlp_kernel(*refs, tiles=tiles, deep=deep), steps,
         [
@@ -1211,11 +1210,11 @@
     quarters = 4
     quarter = width // quarters
     steps = quarters + pairs + 3
-    sum_a = Reduce(sizes, wup, [(0, "0"), (2, "1"), (6, "2"), (9, "3"), (steps, "4")], halves[0])
+    sum_a = Reduce(sizes, wup, [(0, "0"), (2, "1"), (7, "2"), (11, "3"), (steps, "4")], halves[0])
     core = ReduceCore(sizes, wup, [(0, "s"), (3, "w")], halves[1])
-    first = ReduceFirst(sizes, wup, core, [(3, "l"), (4, "a"), (9, "w")], halves[1])
-    second = ReduceSecond(sizes, first, [(9, "l"), (9, "a"), (12, "w")])
-    last_b = ReduceLast(sizes, down_b, [(0, "l"), (1, "a"), (5, "w")])
+    first = ReduceFirst(sizes, wup, core, [(3, "l"), (5, "a"), (11, "w")], halves[1])
+    second = ReduceSecond(sizes, first, [(11, "l"), (12, "a"), (steps, "w")])
+    last_b = ReduceLast(sizes, down_b, [(0, "l"), (1, "a"), (9, "w")])
     pair_b = pl.BlockSpec((count, LANE), turn(quarters, pairs, lambda i: (0, i)))
     table_once = held((count, LANE))
     wout, d_projected, bqkv, wqkv, *moved = run(

time: 428 us -> 422 us (0.986)
  no operation moved by 1% of the time
where the time goes in v2:
time: 422 us; the launch traced here: 416 us
  Pallas kernels  378 us (90%)
  local copies, waits for them, and re-layouts  21.5 us (5%)
  other arithmetic  12.9 us (3%)
    pallas_call x7, Pallas kernels, run(): pl.pallas_call(body, grid=(grid,), in_specs=all_specs, out_specs=all_out_...  378 us

profile of v2, /device:TPU:0, one launch (start us, length us, event | category | flops | bytes accessed | tf_op | source)
XLA Modules:
  0.0 416.3 jit_solution(4840513085654829119)
XLA Ops:
  0.6 0.8 select_reduce_fusion.5
  1.4 0.1 convert_reduce_fusion.1
  1.5 0.7 fusion.19
  2.2 0.2 select_reduce_fusion.4
  2.4 0.7 broadcast_compare_fusion
  3.1 0.1 select_reduce_fusion.3
  3.2 0.1 select_reduce_fusion
  3.3 0.1 broadcast_multiply_fusion.1
  3.4 0.7 tile.4
  4.1 0.1 tile.10
  4.2 3.4 concatenate.21
  7.6 0.6 pad_bitcast_fusion.refs_2_
  8.2 0.5 fusion.6
  8.7 1.5 select_convert_fusion.refs_6_.refs_8_
  10.2 0.9 compare_convert_fusion.refs_7_
  11.2 0.2 copy.50
  11.4 0.2 copy.46
  11.6 1.9 pad_maximum_fusion
  13.5 65.3 %head.1 = (f32[4,8,16,128]{3,2,1,0:T(8,128)}, bf16[2,2,4,2,32,3072]{5,4,3,2,1,0:T(8,128)(2,1)}, bf16[2,2,4,2,32,1024]{5,4,3,2,1,0:T(8,128)(2,1)}, bf16[2,2,4,2,32,4096]{5,4,3,2,1,0:T(8,128)(2,1)}, f32[8,3072]{1,0:T(8,128)}) custom-call(bf16[32,1000]{1,0:T(8,128)(2,1)} %refs_0_.2, bf16[32,6144]{1,0:T(8,128)(2,1)} %refs_1_.1, ...), custom_call_target="tpu_custom_call" | custom-call | bytes 914432 | tf_op jit(solution)/shard_map/head/pallas_call | solution.py:983
  78.8 0.9 reshape.186
  79.7 0.1 copy.61
  79.8 0.1 reshape.187
  79.9 1.0 copy.60
  81.0 0.7 slice.56
  81.6 0.1 slice.54
  81.7 0.7 reshape.190.refs_3_
  82.4 0.1 fusion.21
  82.5 0.7 reshape.194.refs_2_
  83.2 0.1 add.69
  83.2 0.7 broadcast_add_fusion.refs_1_.refs_9_.refs_5_.refs_8_.refs_4_
  83.9 0.7 reshape.191.refs_10_
  84.6 0.1 reshape.204
  84.7 0.1 convert_element_type.75
  84.8 0.3 fusion.2
  85.1 95.9 %fwd.1 = (bf16[1024,1024]{1,0:T(8,128)(2,1)}, bf16[1024,1024]{1,0:T(8,128)(2,1)}, bf16[1024,1024]{1,0:T(8,128)(2,1)}, bf16[1024,1024]{1,0:T(8,128)(2,1)}, bf16[1...) custom-call(bf16[1024,1024]{1,0:T(8,128)(2,1)} %refs_2_.1, ...), custom_call_target="tpu_custom_call", output_to_operand_aliasing={{11}: (12, {}), {12}: (13, {})} | custom-call | bytes 24576000 | tf_op jit(solution)/shard_map/fwd/pallas_call | solution.py:983
  181.0 19.0 %down.1 = (bf16[1024,1024]{1,0:T(8,128)(2,1)}, bf16[1024,1024]{1,0:T(8,128)(2,1)}, f32[4,1024]{1,0:T(4,128)}, f32[1,1024]{1,0:T(1,128)}) custom-call(bf16[1024,4096]{1,0:T(8,128)(2,1)} %get-tuple-element.66.refs_0_, bf16[4096,1024]{1,0:T(8,128)(2,1)} %bitcast.55, f32[1,1024]{1,0:T(1,128)} %reshape.194.refs_2_, ...), custom_call_target="tpu_custom_call" | custom-call | bytes 46342144 | tf_op jit(solution)/shard_map/down/pallas_call | solution.py:983
  199.9 14.4 %wdown.1 = bf16[4096,1024]{1,0:T(8,128)(2,1)} custom-call(bf16[1024,4096]{1,0:T(8,128)(2,1)} %get-tuple-element.66.refs_0_, bf16[1024,1024]{1,0:T(8,128)(2,1)} %get-tuple-element.70.refs_1_.refs_0_), custom_call_target="tpu_custom_call" | custom-call | bytes 20971520 | tf_op jit(solution)/shard_map/wdown/pallas_call | solution.py:983
  214.3 56.4 %mlpb.1 = (f32[1,4096]{1,0:T(1,128)}, bf16[1024,4096]{1,0:T(8,128)(2,1)}, f32[1024,1024]{1,0:T(8,128)}, bf16[1024,1024]{1,0:T(8,128)(2,1)}, f32[4,3,1024]{2,1,0:...) custom-call(bf16[1024,1024]{1,0:T(8,128)(2,1)} %get-tuple-element.70, ...), custom_call_target="tpu_custom_call" | custom-call | bytes 75694080 | tf_op jit(solution)/shard_map/mlpb/pallas_call | solution.py:983
  270.8 66.9 %attb.1 = (bf16[1024,1024]{1,0:T(8,128)(2,1)}, bf16[3,1024,1024]{2,1,0:T(8,128)(2,1)}, f32[8,3,128]{2,1,0:T(4,128)}, bf16[3,1024,1024]{2,1,0:T(8,128)(2,1)}, f32...) custom-call(bf16[1024,1024]{1,0:T(8,128)(2,1)} %get-tuple-element.75, ...), custom_call_target="tpu_custom_call" | custom-call | bytes 40370176 | tf_op jit(solution)/shard_map/attb/pallas_call | solution.py:983
  337.7 0.5 broadcast.174
  338.2 0.7 reduce.6
  338.9 0.7 reduce.7
  339.6 0.1 reshape.201
  339.6 0.1 reshape.203
  339.7 0.7 copy.53
  340.4 0.1 reshape_reshape.6
  340.5 0.1 fusion.5
  340.6 0.7 copy.56
  341.3 59.6 %dact1.1 = (bf16[1024,1024]{1,0:T(8,128)(2,1)}, f32[4,2,1024]{2,1,0:T(2,128)}, f32[32,3072]{1,0:T(8,128)}, f32[32,1024]{1,0:T(8,128)}, bf16[2,2,4,2,24,1024]{5,4...) custom-call(bf16[3,1024,1024]{2,1,0:T(8,128)(2,1)} %get-tuple-element.87.refs_0_, ...), custom_call_target="tpu_custom_call" | custom-call | bytes 38076416 | tf_op jit(solution)/shard_map/dact1/pallas_call | solution.py:983
  400.9 1.3 slice.48
  402.2 1.2 slice_bitcast_fusion
  403.4 1.3 fusion.22
  404.8 1.8 pad_maximum_fusion.2
  406.5 0.8 pad_maximum_fusion.3
  407.4 0.6 reshape.205
  408.0 0.7 copy.54
  408.7 1.0 copy.57
  409.7 0.7 convert_reduce_fusion
  410.4 0.6 fusion
  411.1 1.2 fusion.8
  412.3 1.0 fusion.1
  413.3 1.3 copy.67
  414.6 0.7 copy.68
  415.4 0.7 copy.69
  (36 shorter events, 0.2 us)
Async XLA Ops:
  13.5 71.3 %copy-start.8 = (bf16[32,1000]{1,0:T(8,128)(2,1)S(1)}, bf16[32,1000]{1,0:T(8,128)(2,1)}, u32[]{:S(2)}) copy-start(bf16[32,1000]{1,0:T(8,128)(2,1)} %refs_0_.2) | copy-start | bytes 192004
  270.7 67.5 %copy-start.10 = (f32[1,1024]{1,0:T(1,128)S(1)}, f32[1,1024]{1,0:T(1,128)}, u32[]{:S(2)}) copy-start(f32[1,1024]{1,0:T(1,128)} %get-tuple-element.99) | copy-start | bytes 12292
  270.7 68.1 %copy-start.11 = (f32[1,1024]{1,0:T(1,128)S(1)}, f32[1,1024]{1,0:T(1,128)}, u32[]{:S(2)}) copy-start(f32[1,1024]{1,0:T(1,128)} %get-tuple-element.97) | copy-start | bytes 12292
  270.8 69.8 %copy-start.9 = (f32[1,4096]{1,0:T(1,128)S(1)}, f32[1,4096]{1,0:T(1,128)}, u32[]{:S(2)}) copy-start(f32[1,4096]{1,0:T(1,128)} %get-tuple-element.98) | copy-start | bytes 49156
  341.3 63.5 %copy-start.6 = (f32[32,2048]{1,0:T(8,128)S(1)}, f32[32,2048]{1,0:T(8,128)}, u32[]{:S(2)}) copy-start(f32[32,2048]{1,0:T(8,128)} %get-tuple-element.105) | copy-start | bytes 786436
  341.3 65.3 %copy-start.4 = (f32[128,512]{1,0:T(8,128)S(1)}, f32[128,512]{1,0:T(8,128)}, u32[]{:S(2)}) copy-start(f32[128,512]{1,0:T(8,128)} %get-tuple-element.107) | copy-start | bytes 786436
  341.3 65.3 %copy-start.5 = (f32[128,512]{1,0:T(8,128)S(1)}, f32[128,512]{1,0:T(8,128)}, u32[]{:S(2)}) copy-start(f32[128,512]{1,0:T(8,128)} %get-tuple-element.108) | copy-start | bytes 786436
  400.9 6.5 %copy-start.1 = (bf16[2,2,4,2,24,1024]{5,4,3,2,1,0:T(8,128)(2,1)S(1)}, bf16[2,2,4,2,24,1024]{5,4,3,2,1,0:T(8,128)(2,1)}, u32[]{:S(2)}) copy-start(bf16[2,2,4,2,24,1024]{5,4,3,2,1,0:T(8,128)(2,1)} %get-tuple-element.101) | copy-start | bytes 4718596
  408.7 1.7 copy-start.2
  410.4 2.9 copy-start
  413.3 1.3 copy-start.3
  413.3 2.1 copy-start.7

commit v3 on v2

--- a/solution.py
+++ b/solution.py
@@ -1277,9 +1277,9 @@
         [acc, pltpu.VMEM(mod_block.shape, bf16)], name="dact1",
         moves=[d_mod, q, k, v, oa, ob, last_b, bias], sizes=sizes, group=8,
         script=[
-            (bias, "0"), pack_modulation, (d_mod, "s0"), (v, "2"), (k, "3"), (ob, "1"), (bias, "1"), (oa, "2"), (v, "3"),
-            (d_mod, "n0"), (ob, "2"), (bias, "2"), (oa, "3"), (ob, "3"), (d_mod, "n1"), (bias, "3"), (q, "4"), (k, "4"),
-            (d_mod, "n2"), (bias, "4"), (v, "4"), (d_mod, "w3"), (oa, "4"), (ob, "4"),
+            (bias, "0"), pack_modulation, (d_mod, "s0"), (v, "2"), (k, "3"), (ob, "1"), (bias, "1"), (d_mod, "n0"), (oa, "2"),
+            (v, "3"), (ob, "2"), (bias, "2"), (d_mod, "n1"), (oa, "3"), (ob, "3"), (d_mod, "n2"), (bias, "3"), (q, "4"),
+            (k, "4"), (bias, "4"), (v, "4"), (d_mod, "w3"), (oa, "4"), (ob, "4"),
         ],
     )
     d_mod, wup_high, bias_sum = moved

time: 422 us -> 421 us (level)
  no operation moved by 1% of the time
where the time goes in v3:
time: 421 us; the launch traced here: 416 us
  Pallas kernels  377 us (90%)
  local copies, waits for them, and re-layouts  21.5 us (5%)
  other arithmetic  12.9 us (3%)
    pallas_call x7, Pallas kernels, run(): pl.pallas_call(body, grid=(grid,), in_specs=all_specs, out_specs=all_out_...  377 us

profile of v3, /device:TPU:0, one launch (start us, length us, event | category | flops | bytes accessed | tf_op | source)
XLA Modules:
  0.0 415.7 jit_solution(8384024512376689623)
XLA Ops:
  0.6 0.8 select_reduce_fusion.5
  1.4 0.1 convert_reduce_fusion.1
  1.5 0.7 fusion.19
  2.2 0.2 select_reduce_fusion.4
  2.4 0.7 broadcast_compare_fusion
  3.1 0.1 select_reduce_fusion.3
  3.2 0.1 select_reduce_fusion
  3.3 0.1 broadcast_multiply_fusion.1
  3.4 0.7 tile.4
  4.1 0.1 tile.10
  4.2 3.4 concatenate.21
  7.6 0.6 pad_bitcast_fusion.refs_2_
  8.2 0.5 fusion.6
  8.7 1.5 select_convert_fusion.refs_6_.refs_8_
  10.2 0.9 compare_convert_fusion.refs_7_
  11.2 0.2 copy.50
  11.4 0.2 copy.46
  11.6 1.9 pad_maximum_fusion
  13.5 65.3 %head.1 = (f32[4,8,16,128]{3,2,1,0:T(8,128)}, bf16[2,2,4,2,32,3072]{5,4,3,2,1,0:T(8,128)(2,1)}, bf16[2,2,4,2,32,1024]{5,4,3,2,1,0:T(8,128)(2,1)}, bf16[2,2,4,2,32,4096]{5,4,3,2,1,0:T(8,128)(2,1)}, f32[8,3072]{1,0:T(8,128)}) custom-call(bf16[32,1000]{1,0:T(8,128)(2,1)} %refs_0_.2, bf16[32,6144]{1,0:T(8,128)(2,1)} %refs_1_.1, ...), custom_call_target="tpu_custom_call" | custom-call | bytes 914432 | tf_op jit(solution)/shard_map/head/pallas_call | solution.py:983
  78.8 0.9 reshape.186
  79.7 0.1 copy.61
  79.8 0.1 reshape.187
  79.9 1.0 copy.60
  81.0 0.7 slice.56
  81.6 0.1 slice.54
  81.7 0.7 reshape.190.refs_3_
  82.4 0.1 fusion.21
  82.5 0.7 reshape.194.refs_2_
  83.2 0.1 add.69
  83.2 0.7 broadcast_add_fusion.refs_1_.refs_9_.refs_5_.refs_8_.refs_4_
  83.9 0.7 reshape.191.refs_10_
  84.6 0.1 reshape.204
  84.7 0.1 convert_element_type.75
  84.8 0.3 fusion.2
  85.1 95.9 %fwd.1 = (bf16[1024,1024]{1,0:T(8,128)(2,1)}, bf16[1024,1024]{1,0:T(8,128)(2,1)}, bf16[1024,1024]{1,0:T(8,128)(2,1)}, bf16[1024,1024]{1,0:T(8,128)(2,1)}, bf16[1...) custom-call(bf16[1024,1024]{1,0:T(8,128)(2,1)} %refs_2_.1, ...), custom_call_target="tpu_custom_call", output_to_operand_aliasing={{11}: (12, {}), {12}: (13, {})} | custom-call | bytes 24576000 | tf_op jit(solution)/shard_map/fwd/pallas_call | solution.py:983
  181.0 19.0 %down.1 = (bf16[1024,1024]{1,0:T(8,128)(2,1)}, bf16[1024,1024]{1,0:T(8,128)(2,1)}, f32[4,1024]{1,0:T(4,128)}, f32[1,1024]{1,0:T(1,128)}) custom-call(bf16[1024,4096]{1,0:T(8,128)(2,1)} %get-tuple-element.66.refs_0_, bf16[4096,1024]{1,0:T(8,128)(2,1)} %bitcast.55, f32[1,1024]{1,0:T(1,128)} %reshape.194.refs_2_, ...), custom_call_target="tpu_custom_call" | custom-call | bytes 46342144 | tf_op jit(solution)/shard_map/down/pallas_call | solution.py:983
  199.9 14.4 %wdown.1 = bf16[4096,1024]{1,0:T(8,128)(2,1)} custom-call(bf16[1024,4096]{1,0:T(8,128)(2,1)} %get-tuple-element.66.refs_0_, bf16[1024,1024]{1,0:T(8,128)(2,1)} %get-tuple-element.70.refs_1_.refs_0_), custom_call_target="tpu_custom_call" | custom-call | bytes 20971520 | tf_op jit(solution)/shard_map/wdown/pallas_call | solution.py:983
  214.3 56.4 %mlpb.1 = (f32[1,4096]{1,0:T(1,128)}, bf16[1024,4096]{1,0:T(8,128)(2,1)}, f32[1024,1024]{1,0:T(8,128)}, bf16[1024,1024]{1,0:T(8,128)(2,1)}, f32[4,3,1024]{2,1,0:...) custom-call(bf16[1024,1024]{1,0:T(8,128)(2,1)} %get-tuple-element.70, ...), custom_call_target="tpu_custom_call" | custom-call | bytes 75694080 | tf_op jit(solution)/shard_map/mlpb/pallas_call | solution.py:983
  270.8 66.9 %attb.1 = (bf16[1024,1024]{1,0:T(8,128)(2,1)}, bf16[3,1024,1024]{2,1,0:T(8,128)(2,1)}, f32[8,3,128]{2,1,0:T(4,128)}, bf16[3,1024,1024]{2,1,0:T(8,128)(2,1)}, f32...) custom-call(bf16[1024,1024]{1,0:T(8,128)(2,1)} %get-tuple-element.75, ...), custom_call_target="tpu_custom_call" | custom-call | bytes 40370176 | tf_op jit(solution)/shard_map/attb/pallas_call | solution.py:983
  337.7 0.5 broadcast.174
  338.2 0.7 reduce.6
  338.9 0.7 reduce.7
  339.6 0.1 reshape.201
  339.6 0.1 reshape.203
  339.7 0.7 copy.53
  340.4 0.1 reshape_reshape.6
  340.5 0.1 fusion.5
  340.6 0.7 copy.56
  341.3 59.0 %dact1.1 = (bf16[1024,1024]{1,0:T(8,128)(2,1)}, f32[4,2,1024]{2,1,0:T(2,128)}, f32[32,3072]{1,0:T(8,128)}, f32[32,1024]{1,0:T(8,128)}, bf16[2,2,4,2,24,1024]{5,4...) custom-call(bf16[3,1024,1024]{2,1,0:T(8,128)(2,1)} %get-tuple-element.87.refs_0_, ...), custom_call_target="tpu_custom_call" | custom-call | bytes 38076416 | tf_op jit(solution)/shard_map/dact1/pallas_call | solution.py:983
  400.3 1.3 slice.48
  401.6 1.2 slice_bitcast_fusion
  402.8 1.3 fusion.22
  404.2 1.8 pad_maximum_fusion.2
  406.0 0.8 pad_maximum_fusion.3
  406.8 0.6 reshape.205
  407.4 0.7 copy.54
  408.1 1.0 copy.57
  409.2 0.7 convert_reduce_fusion
  409.9 0.6 fusion
  410.5 1.2 fusion.8
  411.7 1.0 fusion.1
  412.7 1.3 copy.67
  414.1 0.7 copy.68
  414.8 0.7 copy.69
  (36 shorter events, 0.2 us)
Async XLA Ops:
  13.5 71.3 %copy-start.8 = (bf16[32,1000]{1,0:T(8,128)(2,1)S(1)}, bf16[32,1000]{1,0:T(8,128)(2,1)}, u32[]{:S(2)}) copy-start(bf16[32,1000]{1,0:T(8,128)(2,1)} %refs_0_.2) | copy-start | bytes 192004
  270.7 67.5 %copy-start.10 = (f32[1,1024]{1,0:T(1,128)S(1)}, f32[1,1024]{1,0:T(1,128)}, u32[]{:S(2)}) copy-start(f32[1,1024]{1,0:T(1,128)} %get-tuple-element.99) | copy-start | bytes 12292
  270.7 68.1 %copy-start.11 = (f32[1,1024]{1,0:T(1,128)S(1)}, f32[1,1024]{1,0:T(1,128)}, u32[]{:S(2)}) copy-start(f32[1,1024]{1,0:T(1,128)} %get-tuple-element.97) | copy-start | bytes 12292
  270.8 69.8 %copy-start.9 = (f32[1,4096]{1,0:T(1,128)S(1)}, f32[1,4096]{1,0:T(1,128)}, u32[]{:S(2)}) copy-start(f32[1,4096]{1,0:T(1,128)} %get-tuple-element.98) | copy-start | bytes 49156
  341.3 62.9 %copy-start.6 = (f32[32,2048]{1,0:T(8,128)S(1)}, f32[32,2048]{1,0:T(8,128)}, u32[]{:S(2)}) copy-start(f32[32,2048]{1,0:T(8,128)} %get-tuple-element.105) | copy-start | bytes 786436
  341.3 64.7 %copy-start.4 = (f32[128,512]{1,0:T(8,128)S(1)}, f32[128,512]{1,0:T(8,128)}, u32[]{:S(2)}) copy-start(f32[128,512]{1,0:T(8,128)} %get-tuple-element.107) | copy-start | bytes 786436
  341.3 64.7 %copy-start.5 = (f32[128,512]{1,0:T(8,128)S(1)}, f32[128,512]{1,0:T(8,128)}, u32[]{:S(2)}) copy-start(f32[128,512]{1,0:T(8,128)} %get-tuple-element.108) | copy-start | bytes 786436
  400.3 6.5 %copy-start.1 = (bf16[2,2,4,2,24,1024]{5,4,3,2,1,0:T(8,128)(2,1)S(1)}, bf16[2,2,4,2,24,1024]{5,4,3,2,1,0:T(8,128)(2,1)}, u32[]{:S(2)}) copy-start(bf16[2,2,4,2,24,1024]{5,4,3,2,1,0:T(8,128)(2,1)} %get-tuple-element.101) | copy-start | bytes 4718596
  408.1 1.7 copy-start.2
  409.9 2.9 copy-start
  412.7 1.3 copy-start.3
  412.7 2.1 copy-start.7
